TPU v7x, 256 devices: a whole 4x4x8 slice. The times are simulated.
256 devices in a mesh: seq: 64 (over x_hi, y, z), doc: 4 (over x_lo, core).
Axes of the slice: x: 4 (x_hi: 2, x_lo: 2; x = x_hi * 2 + x_lo), y: 4, z: 8, core: 2. Of those that a mesh axis runs over, the one named last changes fastest.
Arguments:
- tokens: bfloat16 [4, 8192, 4096], P('doc', 'seq'), may hold values from -6 to 6
- norm_gain: float32 [4096], replicated, may hold values from 0.5 to 9
- w_query: bfloat16 [4096, 2048], P(None, 'doc'), may hold values from -0.09375 to 0.09375
- key_weight: bfloat16 [4096, 512], P(None, 'doc'), may hold values from -0.09375 to 0.09375
- value_weight: bfloat16 [4096, 512], P(None, 'doc'), may hold values from -0.09375 to 0.09375
- vertical_blocks: int32 [4, 4, 4], replicated, may hold values from 0 to 63, as said below
- slash_offsets: int32 [4, 4, 4], replicated, may hold values from 2 to 63, as said below
Outputs:
- attended: bfloat16 [4, 8192, 2048], P('doc', 'seq')
Inputs may be any that keep to these rules, and one draw needn't show every extreme that they name: `vertical_blocks`: within one document and key-value head the 4 block indices are distinct. `slash_offsets`: within one document and key-value head the 4 offsets are distinct.
All inputs are finite; a program needn't handle non-finite values.
Results may differ from a plain program's by a relative error of at most 0.013.
The roundings to bfloat16 on the way count: a program that leaves them out, or rounds other values in their place, can miss the bound.
Values may be sent and summed in bfloat16 or wider, within the bound.
A program may use at most 64 MiB of HBM per device.

v0:
```python
import jax
import jax.numpy as jnp
from jax import lax
from jax.sharding import PartitionSpec as P

QUERY_HEADS = 16
KEY_VALUE_HEADS = 4
HEAD_WIDTH = 128


def from_behind(value, axis, steps):
    count = lax.axis_size(axis)
    initial, last = (max(0, -steps), min(count, count - steps))
    return lax.ppermute(value, axis, [(source, source + steps) for source in range(initial, last)])


def rope_table(positions, width):
    inverse = jnp.power(jnp.float32(500000.0), -jnp.arange(0, width, 2, dtype=jnp.float32) / width)
    angles = positions.astype(jnp.float32)[:, None] * inverse[None, :]
    return (jnp.cos(angles), jnp.sin(angles))


def apply_rotation(value_rows, cosine_table, sine_table):
    half = value_rows.shape[-1] // 2
    first = value_rows[..., :half]
    second = value_rows[..., half:]
    cosine_table = cosine_table[:, None, :]
    sine_table = sine_table[:, None, :]
    return jnp.concatenate(
        [first * cosine_table - second * sine_table, second * cosine_table + first * sine_table],
        axis=-1,
    )


def normalize(tokens, norm_gain):
    widened = tokens.astype(jnp.float32)
    scale = lax.rsqrt(jnp.mean(widened * widened, axis=-1, keepdims=True) + 1e-05)
    return (widened * scale * norm_gain).astype(jnp.bfloat16)


def slot_masks(rows, slots):
    query_index = jnp.arange(rows)[:, None, None]
    key_index = jnp.arange(rows)[None, None, :]
    slot_index = jnp.arange(slots)[None, :, None]
    return (slot_index > 0) | (key_index <= query_index)


def block_validity(place, vertical, offsets):
    slash_index = place - offsets
    repeated = jnp.any(vertical[..., :, None] == slash_index[..., None, :], axis=-1)
    own = jnp.ones(slash_index.shape[:-1] + (1,), dtype=jnp.bool_)
    previous = jnp.broadcast_to(place >= 1, own.shape)
    return jnp.concatenate(
        [own, previous, slash_index >= 0, (vertical < place - 1) & ~repeated], axis=-1
    )


def attend(query_rows, keys_all, valid, masks):
    width = query_rows.shape[-1]
    scores = jnp.einsum(
        "lqhgd,lskhd->lhgqsk", query_rows, keys_all[..., :width], preferred_element_type=jnp.float32
    ) * width ** (-0.5)
    mask = valid[:, :, None, None, :, None] & masks[None, None, None]
    scores = jnp.where(mask, scores, -jnp.inf)
    highest = jnp.max(scores, axis=(4, 5), keepdims=True)
    raised = jnp.exp(scores - highest)
    total = jnp.sum(raised, axis=(4, 5))
    weights = raised.astype(jnp.bfloat16)
    mixed_output = jnp.einsum(
        "lhgqsk,lskhd->lqhgd", weights, keys_all[..., width:], preferred_element_type=jnp.float32
    )
    mixed_output = mixed_output / jnp.transpose(total, (0, 3, 1, 2))[..., None]
    return mixed_output.astype(jnp.bfloat16).reshape(query_rows.shape[0], query_rows.shape[1], -1)


def local(tokens, norm_gain, w_query, key_weight, value_weight, vertical_blocks, slash_offsets):
    local_docs, rows, width = tokens.shape
    query_group = QUERY_HEADS // KEY_VALUE_HEADS
    place = lax.axis_index("seq")
    doc_place = lax.axis_index("doc")
    normed_input = normalize(tokens, norm_gain)
    cosine_table, sine_table = rope_table(
        place * rows + jnp.arange(rows, dtype=jnp.int32), HEAD_WIDTH
    )
    local_heads = key_weight.shape[1] // HEAD_WIDTH
    query_cols = local_heads * query_group * HEAD_WIDTH
    piece = lax.all_gather(normed_input, "doc", axis=0, tiled=True)
    amount = piece.shape[0]
    flat = piece.reshape(amount * rows, width)
    query_part = jnp.dot(flat, w_query, preferred_element_type=jnp.float32).reshape(
        amount, rows, local_heads * query_group, HEAD_WIDTH
    )
    key_part = jnp.dot(flat, key_weight, preferred_element_type=jnp.float32).reshape(
        amount, rows, local_heads, HEAD_WIDTH
    )
    value_part = jnp.dot(flat, value_weight, preferred_element_type=jnp.float32).reshape(
        amount, rows, local_heads, HEAD_WIDTH
    )
    query_part = (
        apply_rotation(query_part, cosine_table, sine_table)
        .astype(jnp.bfloat16)
        .reshape(amount, rows, query_cols)
    )
    joined = jnp.concatenate(
        [
            apply_rotation(key_part, cosine_table, sine_table).astype(jnp.bfloat16),
            value_part.astype(jnp.bfloat16),
        ],
        axis=-1,
    )
    projected = jnp.concatenate(
        [query_part, joined.reshape(amount, rows, local_heads * 2 * HEAD_WIDTH)], axis=-1
    )
    lanes = projected.shape[0]
    query_rows = projected[:, :, :query_cols].reshape(
        lanes, rows, local_heads, query_group, HEAD_WIDTH
    )
    key_value = projected[:, :, query_cols:].reshape(lanes, rows, local_heads, 2 * HEAD_WIDTH)
    vertical = lax.dynamic_slice_in_dim(vertical_blocks, doc_place * local_heads, local_heads, 1)
    offsets = lax.dynamic_slice_in_dim(slash_offsets, doc_place * local_heads, local_heads, 1)
    lanes = key_value.shape[0]
    slash_count = offsets.shape[2]
    previous = from_behind(key_value, "seq", 1)
    spread = jnp.broadcast_to(key_value[:, None], (lanes, slash_count) + key_value.shape[1:])
    for level in range(lax.axis_size("seq").bit_length() - 1):
        moved = from_behind(spread, "seq", 1 << level)
        chosen = jnp.right_shift(offsets, level) % 2 == 1
        spread = jnp.where(jnp.transpose(chosen, (0, 2, 1))[:, :, None, :, None], moved, spread)
    owned = jnp.transpose(vertical == place, (0, 2, 1))[:, :, None, :, None]
    picked = jnp.where(owned, key_value[:, None].astype(jnp.float32), jnp.zeros((), jnp.float32))
    far_keys = lax.psum(picked, "seq").astype(jnp.bfloat16)
    keys_all = jnp.concatenate([key_value[:, None], previous[:, None], spread, far_keys], axis=1)
    valid = block_validity(place, vertical, offsets)
    mixed_output = attend(query_rows, keys_all, valid, slot_masks(rows, keys_all.shape[1]))
    return lax.all_to_all(mixed_output, "doc", split_axis=0, concat_axis=2, tiled=True)


def solution(mesh):
    return jax.shard_map(
        local,
        mesh=mesh,
        in_specs=(
            P("doc", "seq", None),
            P(),
            P(None, "doc"),
            P(None, "doc"),
            P(None, "doc"),
            P(),
            P(),
        ),
        out_specs=P("doc", "seq", None),
        check_vma=False,
    )
```

profile of v0, /device:TPU:5, one launch (start us, length us, event | category | flops | bytes accessed | tf_op | source)
XLA Modules:
  0.0 698.7 jit_solution(3999746179824464056)
XLA Ops:
  6.5 0.0 copy-start
  6.5 0.0 all-gather.2.cloned.1.call-start
  6.5 1.6 fusion.9
  8.2 0.0 copy-start.4
  8.2 2.6 fusion.11
  10.8 0.0 all-gather.2.cloned.1.call-update
  10.8 0.2 multiply_cosine_fusion
  11.0 52.0 %all-gather.2.cloned.1.call-done = bf16[4,128,4096]{2,1,0:T(8,128)(2,1)} async-done(((bf16[1,128,4096]{2,1,0:T(8,128)(2,1)}), bf16[4,128,4096]{2,1,0:T(8,128)(2,1)}) %all-gather.2.cloned.1.call-update) | async-done | bytes 4194320 | tf_op jit(solution)/shard_map/all_gather | solution.py:87
  63.0 0.0 copy-done
  63.1 3.8 convolution_bitcast_fusion
  67.0 0.0 copy-done.4
  67.0 0.0 copy-done.1
  67.0 1.5 fusion.16
  68.5 1.0 fusion.45
  69.5 0.1 copy.37
  69.6 1.1 broadcast_in_dim.119
  70.7 3.2 collective-permute-start.1
  73.9 0.7 constant_dynamic-slice_fusion
  74.6 29.0 %collective-permute-done.1 = bf16[4,4,128,1,256]{4,2,1,0,3:T(8,128)(2,1)S(1)} collective-permute-done((bf16[4,4,128,1,256]{4,2,1,0,3:T(8,128)(2,1)}, bf16[4,4,128,1,256]{4,2,1,0,3:T(8,128)(2,1)S(1)}, u32[]{:S(2)}, u32[]{:S(2)}) %collective-permute-start.1) | collective-permute-done | bytes 1048608 | tf_op jit(solution)/shard_map/ppermute | solution.py:14
  103.7 0.1 broadcast_select_fusion.1
  103.8 1.9 collective-permute-start.2
  105.8 50.1 %collective-permute-done.2 = bf16[4,4,128,1,256]{4,2,1,0,3:T(8,128)(2,1)S(1)} collective-permute-done((bf16[4,4,128,1,256]{4,2,1,0,3:T(8,128)(2,1)S(1)}, bf16[4,4,128,1,256]{4,2,1,0,3:T(8,128)(2,1)S(1)}, u32[]{:S(2)}, u32[]{:S(2)}) %collective-permute-start.2) | collective-permute-done | bytes 1048608 | tf_op jit(solution)/shard_map/ppermute | solution.py:14
  155.8 0.4 broadcast_select_fusion.2
  156.2 1.9 collective-permute-start.3
  158.1 52.9 %collective-permute-done.3 = bf16[4,4,128,1,256]{4,2,1,0,3:T(8,128)(2,1)S(1)} collective-permute-done((bf16[4,4,128,1,256]{4,2,1,0,3:T(8,128)(2,1)S(1)}, bf16[4,4,128,1,256]{4,2,1,0,3:T(8,128)(2,1)S(1)}, u32[]{:S(2)}, u32[]{:S(2)}) %collective-permute-start.3) | collective-permute-done | bytes 1048608 | tf_op jit(solution)/shard_map/ppermute | solution.py:14
  211.0 0.2 broadcast_select_fusion.3
  211.2 1.9 collective-permute-start.4
  213.1 6.5 copy.59
  219.7 0.2 compare_reduce_fusion
  219.9 21.0 %collective-permute-done.4 = bf16[4,4,128,1,256]{4,2,1,0,3:T(8,128)(2,1)} collective-permute-done((bf16[4,4,128,1,256]{4,2,1,0,3:T(8,128)(2,1)S(1)}, bf16[4,4,128,1,256]{4,2,1,0,3:T(8,128)(2,1)}, u32[]{:S(2)}, u32[]{:S(2)}) %collective-permute-start.4) | collective-permute-done | bytes 1048608 | tf_op jit(solution)/shard_map/ppermute | solution.py:14
  241.0 2.4 broadcast_select_fusion.4
  243.3 1.9 collective-permute-start.5
  245.3 0.1 pad_add_fusion
  245.3 0.1 add_bitcast_fusion
  245.4 0.1 broadcast_or_fusion
  245.6 1.2 broadcast_and_fusion
  246.8 10.7 %collective-permute-start = (bf16[4,128,1,256]{1,3,0,2:T(8,128)(2,1)}, bf16[4,128,1,256]{1,3,0,2:T(8,128)(2,1)}, u32[]{:S(2)}, u32[]{:S(2)}) collective-permute-start(bf16[4,128,1,256]{1,3,0,2:T(8,128)(2,1)} %get-tuple-element.12), channel_id=1, source_target_pairs={{0,4},{4,8},{8,12},{12,16},{16,20},{20,24},{24,28},{28,32},{32,36}... | collective-permute-start | bytes 786440 | tf_op jit(solution)/shard_map/ppermute | solution.py:14
  257.4 1.0 copy.39
  258.4 1.3 broadcast_select_fusion
  259.7 18.4 %collective-permute-done.5 = bf16[4,4,128,1,256]{4,2,1,0,3:T(8,128)(2,1)} collective-permute-done((bf16[4,4,128,1,256]{4,2,1,0,3:T(8,128)(2,1)}, bf16[4,4,128,1,256]{4,2,1,0,3:T(8,128)(2,1)}, u32[]{:S(2)}, u32[]{:S(2)}) %collective-permute-start.5) | collective-permute-done | bytes 1048608 | tf_op jit(solution)/shard_map/ppermute | solution.py:14
  278.2 2.7 broadcast_select_fusion.5
  280.9 1.3 collective-permute-start.6
  282.2 323.7 %all-reduce.1 = bf16[4,4,128,1,256]{4,2,1,0,3:T(8,128)(2,1)} all-reduce(f32[4,4,128,1,256]{4,2,1,0,3:T(8,128)S(1)} %broadcast_select_fusion), channel_id=1, replica_groups=mesh['seq'=64,'doc'=4] {'seq'}, use_global_device_ids=true, to_apply=%region_1.2 | all-reduce | flops 524288 | bytes 3145728 | tf_op jit(solution)/shard_map/psum | solution.py:131
  605.9 5.4 fusion.7
  611.4 0.0 copy-start.2
  611.4 1.2 copy.40
  612.5 1.0 subtract_convert_fusion
  613.5 0.0 collective-permute-done
  613.5 1.1 copy.41
  614.6 0.0 collective-permute-done.6
  614.6 0.0 copy-start.3
  614.6 0.0 copy-start.5
  614.6 0.0 copy-start.6
  614.6 1.8 broadcast_select_fusion.6
  616.4 0.0 copy-done.2
  616.5 0.3 pad_maximum_fusion
  616.8 0.0 copy-done.3
  616.8 0.0 copy-done.5
  616.8 0.0 copy-done.6
  616.8 1.7 fusion.2
  618.5 2.5 fusion
  621.0 2.6 divide_convert_fusion
  623.7 67.1 %all_to_all.18 = bf16[4,128,512]{1,2,0:T(8,128)(2,1)S(1)} all-to-all(bf16[4,128,512]{1,2,0:T(8,128)(2,1)S(1)} %bitcast.128), channel_id=1, replica_groups=mesh['seq'=64,'doc'=4] {'doc'}, dimensions={0} | all-to-all | bytes 1048576 | tf_op jit(solution)/shard_map/all_to_all | solution.py:135
  690.8 1.0 copy.63
  (10 shorter events, 0.1 us)
Async XLA Ops:
  6.5 56.5 %copy-start = (bf16[4096,128]{1,0:T(8,128)(2,1)S(1)}, bf16[4096,128]{1,0:T(8,128)(2,1)}, u32[]{:S(2)}) copy-start(bf16[4096,128]{1,0:T(8,128)(2,1)} %param.10) | copy-start | bytes 3145732
  6.5 56.5 %all-gather.2.cloned.1.call-start = ((), (), s32[]{:S(2)}) async-start(), calls=%async_computation.1 | async-start | bytes 5242880 | tf_op jit(solution)/shard_map/all_gather | solution.py:87
  8.2 58.8 %copy-start.4 = (bf16[4096,128]{1,0:T(8,128)(2,1)S(1)}, bf16[4096,128]{1,0:T(8,128)(2,1)}, u32[]{:S(2)}) copy-start(bf16[4096,128]{1,0:T(8,128)(2,1)} %param.11) | copy-start | bytes 3145732
  63.1 3.9 copy-start.1
  70.7 33.0 %collective-permute-start.1 = (bf16[4,4,128,1,256]{4,2,1,0,3:T(8,128)(2,1)}, bf16[4,4,128,1,256]{4,2,1,0,3:T(8,128)(2,1)S(1)}, u32[]{:S(2)}, u32[]{:S(2)}) collective-permute-start(bf16[4,4,128,1,256]{4,2,1,0,3:T(8,128)(2,1)} %broadcast_in_dim.119), channel_id=1, source_target_pairs={{0,4},{4,8},{8,12},{12,16},{16,20},{20,24},{24,28},{28,32},{32,36}... | collective-permute-start | bytes 3145736 | tf_op jit(solution)/shard_map/ppermute | solution.py:14
  103.8 52.0 %collective-permute-start.2 = (bf16[4,4,128,1,256]{4,2,1,0,3:T(8,128)(2,1)S(1)}, bf16[4,4,128,1,256]{4,2,1,0,3:T(8,128)(2,1)S(1)}, u32[]{:S(2)}, u32[]{:S(2)}) collective-permute-start(bf16[4,4,128,1,256]{4,2,1,0,3:T(8,128)(2,1)S(1)} %broadcast_select_fusion.1), channel_id=1, source_target_pairs={{0,8},{4,12},{8,16},{12,20},{16,24},{20,28},{24,32},{28,36},{32,40... | collective-permute-start | bytes 3145736 | tf_op jit(solution)/shard_map/ppermute | solution.py:14
  156.2 54.8 %collective-permute-start.3 = (bf16[4,4,128,1,256]{4,2,1,0,3:T(8,128)(2,1)S(1)}, bf16[4,4,128,1,256]{4,2,1,0,3:T(8,128)(2,1)S(1)}, u32[]{:S(2)}, u32[]{:S(2)}) collective-permute-start(bf16[4,4,128,1,256]{4,2,1,0,3:T(8,128)(2,1)S(1)} %broadcast_select_fusion.2), channel_id=1, source_target_pairs={{0,16},{4,20},{8,24},{12,28},{16,32},{20,36},{24,40},{28,44},{32,4... | collective-permute-start | bytes 3145736 | tf_op jit(solution)/shard_map/ppermute | solution.py:14
  211.2 29.8 %collective-permute-start.4 = (bf16[4,4,128,1,256]{4,2,1,0,3:T(8,128)(2,1)S(1)}, bf16[4,4,128,1,256]{4,2,1,0,3:T(8,128)(2,1)}, u32[]{:S(2)}, u32[]{:S(2)}) collective-permute-start(bf16[4,4,128,1,256]{4,2,1,0,3:T(8,128)(2,1)S(1)} %broadcast_select_fusion.3), channel_id=1, source_target_pairs={{0,32},{4,36},{8,40},{12,44},{16,48},{20,52},{24,56},{28,60},{32,6... | collective-permute-start | bytes 3145736 | tf_op jit(solution)/shard_map/ppermute | solution.py:14
  243.3 34.8 %collective-permute-start.5 = (bf16[4,4,128,1,256]{4,2,1,0,3:T(8,128)(2,1)}, bf16[4,4,128,1,256]{4,2,1,0,3:T(8,128)(2,1)}, u32[]{:S(2)}, u32[]{:S(2)}) collective-permute-start(bf16[4,4,128,1,256]{4,2,1,0,3:T(8,128)(2,1)} %broadcast_select_fusion.4), channel_id=1, source_target_pairs={{0,64},{4,68},{8,72},{12,76},{16,80},{20,84},{24,88},{28,92},{32,9... | collective-permute-start | bytes 3145736 | tf_op jit(solution)/shard_map/ppermute | solution.py:14
  246.8 366.7 %collective-permute-start = (bf16[4,128,1,256]{1,3,0,2:T(8,128)(2,1)}, bf16[4,128,1,256]{1,3,0,2:T(8,128)(2,1)}, u32[]{:S(2)}, u32[]{:S(2)}) collective-permute-start(bf16[4,128,1,256]{1,3,0,2:T(8,128)(2,1)} %get-tuple-element.12), channel_id=1, source_target_pairs={{0,4},{4,8},{8,12},{12,16},{16,20},{20,24},{24,28},{28,32},{32,36}... | collective-permute-start | bytes 786440 | tf_op jit(solution)/shard_map/ppermute | solution.py:14
  280.9 333.7 %collective-permute-start.6 = (bf16[4,4,128,1,256]{4,2,1,0,3:T(8,128)(2,1)}, bf16[4,4,128,1,256]{4,2,1,0,3:T(8,128)(2,1)}, u32[]{:S(2)}, u32[]{:S(2)}) collective-permute-start(bf16[4,4,128,1,256]{4,2,1,0,3:T(8,128)(2,1)} %broadcast_select_fusion.5), channel_id=1, source_target_pairs={{0,128},{4,132},{8,136},{12,140},{16,144},{20,148},{24,152},{28,15... | collective-permute-start | bytes 3145736 | tf_op jit(solution)/shard_map/ppermute | solution.py:14
  611.4 5.1 copy-start.2
  614.6 2.2 copy-start.3
  614.6 2.2 copy-start.5
  614.6 2.2 copy-start.6
Sparse Core Ops, SparseCore 0:
  10.9 52.0 all-gather.1
where the time goes:
time: 700 us; the launch traced here: 699 us
  blocking collectives  391 us (56%)
  waiting for transfers between devices  224 us (32%)
  starting transfers between devices  22.8 us (3%)
  other arithmetic  19.9 us (3%)
  matrix products  15.1 us (2%)
  between operations  13.7 us (2%)
  local copies, waits for them, and re-layouts  12.7 us (2%)
    psum x1, blocking collectives, local(): far_keys = lax.psum(picked, 'seq').astype(jnp.bfloat16)  324 us
    ppermute x7, waiting for transfers between devices, from_behind(): lax.ppermute(value, axis, [(source, source + steps) for source in range(i...  171 us
    all_to_all x1, blocking collectives, local(): lax.all_to_all(mixed_output, 'doc', split_axis=0, concat_axis=2, tiled=True)  67.1 us
    all_gather x1, waiting for transfers between devices, local(): piece = lax.all_gather(normed_input, 'doc', axis=0, tiled=True)  52 us
    ppermute x7, starting transfers between devices, from_behind(): lax.ppermute(value, axis, [(source, source + steps) for source in range(i...  22.8 us
  transfers between devices with their start and end apart: 8, of which 6 were waited for; matrix products, arithmetic and copies ran while one was open for 3% of the time, Pallas kernels for 0%

commit v1 on v0

--- a/solution.py
+++ b/solution.py
@@ -6,12 +6,6 @@
 QUERY_HEADS = 16
 KEY_VALUE_HEADS = 4
 HEAD_WIDTH = 128
-
-
-def from_behind(value, axis, steps):
-    count = lax.axis_size(axis)
-    initial, last = (max(0, -steps), min(count, count - steps))
-    return lax.ppermute(value, axis, [(source, source + steps) for source in range(initial, last)])
 
 
 def rope_table(positions, width):
@@ -119,17 +113,11 @@
     vertical = lax.dynamic_slice_in_dim(vertical_blocks, doc_place * local_heads, local_heads, 1)
     offsets = lax.dynamic_slice_in_dim(slash_offsets, doc_place * local_heads, local_heads, 1)
     lanes = key_value.shape[0]
-    slash_count = offsets.shape[2]
-    previous = from_behind(key_value, "seq", 1)
-    spread = jnp.broadcast_to(key_value[:, None], (lanes, slash_count) + key_value.shape[1:])
-    for level in range(lax.axis_size("seq").bit_length() - 1):
-        moved = from_behind(spread, "seq", 1 << level)
-        chosen = jnp.right_shift(offsets, level) % 2 == 1
-        spread = jnp.where(jnp.transpose(chosen, (0, 2, 1))[:, :, None, :, None], moved, spread)
-    owned = jnp.transpose(vertical == place, (0, 2, 1))[:, :, None, :, None]
-    picked = jnp.where(owned, key_value[:, None].astype(jnp.float32), jnp.zeros((), jnp.float32))
-    far_keys = lax.psum(picked, "seq").astype(jnp.bfloat16)
-    keys_all = jnp.concatenate([key_value[:, None], previous[:, None], spread, far_keys], axis=1)
+    gathered = lax.all_gather(key_value[:, :, 0], "seq", axis=0)
+    near = jnp.broadcast_to(jnp.stack([place, place - 1]), (lanes, 2))
+    chosen = jnp.concatenate([near, place - offsets[:, 0], vertical[:, 0]], axis=1)
+    chosen = jnp.clip(chosen, 0, gathered.shape[0] - 1)
+    keys_all = gathered[chosen, jnp.arange(lanes)[:, None]][:, :, :, None]
     valid = block_validity(place, vertical, offsets)
     mixed_output = attend(query_rows, keys_all, valid, slot_masks(rows, keys_all.shape[1]))
     return lax.all_to_all(mixed_output, "doc", split_axis=0, concat_axis=2, tiled=True)

time: 700 us -> 315 us (0.45)
  blocking collectives: 391 us -> 12.3 us
  starting transfers between devices: 22.8 us -> 0.04 us
  waiting for transfers between devices: 224 us -> 244 us
  other arithmetic: 19.9 us -> 8.3 us
    psum x1 -> x0, blocking collectives: 324 us -> none  [local(): far_keys = lax.psum(picked, 'seq').astype(jnp.bfloat16)]
    all_gather x0 -> x1, waiting for transfers between devices: none -> 192 us  [local(): gathered = lax.all_gather(key_value[:, :, 0], 'seq', axis=0)]
    ppermute x7 -> x0, waiting for transfers between devices: 171 us -> none  [from_behind(): lax.ppermute(value, axis, [(source, source + steps) for source in range(i...]
    all_to_all x1, blocking collectives: 67.1 us -> 12.3 us  [local(): lax.all_to_all(mixed_output, 'doc', split_axis=0, concat_axis=2, tiled=True)]
    ppermute x7 -> x0, starting transfers between devices: 22.8 us -> none  [from_behind(): lax.ppermute(value, axis, [(source, source + steps) for source in range(i...]
    select_n x7 -> x0, other arithmetic: 8.85 us -> none  [the longest x6 7.56 us: local(): jnp.where(jnp.transpose(chosen, (0, 2, 1))[:, :, None, :, None], moved, s...]
    gather x0 -> x1, local copies, waits for them, and re-layouts: none -> 8.13 us  [local(): keys_all = gathered[chosen, jnp.arange(lanes)[:, None]][:, :, :, None]]
  transfers between devices with their start and end apart: 8 -> 2, of which waited for: 6 -> 2; matrix products, arithmetic and copies ran while one was open for 3% -> 5% of each run, Pallas kernels for 0% -> 0%
where the time goes in v1:
time: 315 us; the launch traced here: 312 us
  waiting for transfers between devices  244 us (77%)
  local copies, waits for them, and re-layouts  17.3 us (5%)
  matrix products  16.3 us (5%)
  between operations  13.6 us (4%)
  blocking collectives  12.3 us (4%)
  other arithmetic  8.3 us (3%)
    all_gather x1, waiting for transfers between devices, local(): gathered = lax.all_gather(key_value[:, :, 0], 'seq', axis=0)  192 us
    all_gather x1, waiting for transfers between devices, local(): piece = lax.all_gather(normed_input, 'doc', axis=0, tiled=True)  52 us
    all_to_all x1, blocking collectives, local(): lax.all_to_all(mixed_output, 'doc', split_axis=0, concat_axis=2, tiled=True)  12.3 us
    gather x1, local copies, waits for them, and re-layouts, local(): keys_all = gathered[chosen, jnp.arange(lanes)[:, None]][:, :, :, None]  8.13 us
    dot_general x1, local copies, waits for them, and re-layouts, local(): jnp.dot(flat, w_query, preferred_element_type=jnp.float32)  6.45 us
  transfers between devices with their start and end apart: 2, of which 2 were waited for; matrix products, arithmetic and copies ran while one was open for 5% of the time, Pallas kernels for 0%

profile of v1, /device:TPU:5, one launch (start us, length us, event | category | flops | bytes accessed | tf_op | source)
XLA Modules:
  0.0 312.1 jit_solution(17268956264786893167)
XLA Ops:
  6.5 0.0 copy-start
  6.5 0.0 all-gather.4.cloned.1.call-start
  6.5 1.6 fusion.9
  8.2 0.0 copy-start.3
  8.2 2.6 fusion.11
  10.8 0.0 all-gather.4.cloned.1.call-update
  10.8 0.0 all-gather.6.cloned.1.call-start
  10.9 0.2 multiply_cosine_fusion
  11.1 52.0 %all-gather.4.cloned.1.call-done = bf16[4,128,4096]{2,1,0:T(8,128)(2,1)} async-done(((bf16[1,128,4096]{2,1,0:T(8,128)(2,1)}), bf16[4,128,4096]{2,1,0:T(8,128)(2,1)}) %all-gather.4.cloned.1.call-update) | async-done | bytes 4194320 | tf_op jit(solution)/shard_map/all_gather | solution.py:81
  63.1 0.0 copy-done
  63.1 0.0 copy-start.1
  63.1 3.8 %convolution_bitcast_fusion = f32[4,128,1,128]{1,3,0,2:T(8,128)S(1)} fusion(bf16[4,128,4096]{2,1,0:T(8,128)(2,1)} %all-gather.4.cloned.1.call-done, bf16[4096,128]{1,0:T(8,128)(2,1)S(1)} %copy-done), kind=kOutput, calls=%fused_computation.21 | convolution fusion | flops 536870912 | bytes 5505024 | tf_op jit(solution)/shard_map/dot_general | solution.py:87
  67.0 0.0 copy-done.3
  67.0 0.0 copy-done.1
  67.0 1.5 fusion.16
  68.5 0.9 copy.30
  69.4 0.0 all-gather.6.cloned.1.call-update
  69.4 6.4 %copy.50 = bf16[512,4096]{1,0:T(8,128)(2,1)} copy(bf16[512,4096]{0,1:T(8,128)(2,1)} %bitcast.115) | data formatting | bytes 8388608 | tf_op jit(solution)/shard_map/dot_general | solution.py:84
  75.9 0.1 pad_add_fusion.1
  75.9 0.7 constant_dynamic-slice_fusion
  76.7 0.1 fusion.25
  76.7 0.1 reshape.251
  76.8 0.1 pad_add_fusion
  76.9 0.2 compare_reduce_fusion
  77.2 0.1 add_bitcast_fusion
  77.3 0.1 broadcast_or_fusion
  77.4 0.4 broadcast_and_fusion
  77.8 5.5 %fusion.7 = f32[4,128,4,128]{1,3,2,0:T(8,128)S(1)} fusion(bf16[4,128,4096,1]{2,1,0,3:T(8,128)(2,1)} %bitcast.116, bf16[4,128,4096]{2,1,0:T(8,128)(2,1)} %all-gather.4.cloned.1.call-done), kind=kOutput, calls=%fused_computation.9 | convolution fusion | flops 2147483648 | bytes 9437184 | tf_op jit(solution)/shard_map/dot_general | solution.py:84
  83.3 0.1 subtract_convert_fusion
  83.4 192.3 %all-gather.6.cloned.1.call-done = bf16[256,128,1,256]{3,1,2,0:T(8,128)(2,1)} async-done(((bf16[4,128,1,256]{3,1,2,0:T(8,128)(2,1)}), bf16[256,128,1,256]{3,1,2,0:T(8,128)(2,1)}) %all-gather.6.cloned.1.call-update) | async-done | bytes 16777232 | tf_op jit(solution)/shard_map/all_gather | solution.py:116
  275.7 8.1 %gather_fusion = bf16[40,128,256]{2,1,0:T(8,128)(2,1)} fusion(bf16[64,4,128,256]{3,2,1,0:T(8,128)(2,1)} %bitcast.121, s32[40]{0:T(128)S(1)} %reshape.251), kind=kCustom, calls=%fused_computation | custom fusion | bytes 5243200 | tf_op jit(solution)/shard_map/gather | solution.py:120
  283.9 2.8 fusion.2
  286.7 0.0 copy-start.2
  286.7 2.6 fusion
  289.3 0.0 copy-done.2
  289.3 2.7 divide_convert_fusion
  292.0 12.3 %all_to_all.18 = bf16[4,128,512]{1,2,0:T(8,128)(2,1)S(1)} all-to-all(bf16[4,128,512]{1,2,0:T(8,128)(2,1)S(1)} %bitcast.120), channel_id=1, replica_groups=mesh['seq'=64,'doc'=4] {'doc'}, dimensions={0} | all-to-all | bytes 1048576 | tf_op jit(solution)/shard_map/all_to_all | solution.py:123
  304.3 1.0 copy.54
  (11 shorter events, 0.1 us)
Async XLA Ops:
  6.5 56.5 %copy-start = (bf16[4096,128]{1,0:T(8,128)(2,1)S(1)}, bf16[4096,128]{1,0:T(8,128)(2,1)}, u32[]{:S(2)}) copy-start(bf16[4096,128]{1,0:T(8,128)(2,1)} %param.10) | copy-start | bytes 3145732
  6.5 56.5 %all-gather.4.cloned.1.call-start = ((), (), s32[]{:S(2)}) async-start(), calls=%async_computation.1 | async-start | bytes 5242880 | tf_op jit(solution)/shard_map/all_gather | solution.py:81
  8.2 58.8 %copy-start.3 = (bf16[4096,128]{1,0:T(8,128)(2,1)S(1)}, bf16[4096,128]{1,0:T(8,128)(2,1)}, u32[]{:S(2)}) copy-start(bf16[4096,128]{1,0:T(8,128)(2,1)} %param.11) | copy-start | bytes 3145732
  10.8 264.9 %all-gather.6.cloned.1.call-start = ((), (), s32[]{:S(2)}) async-start(), calls=%async_computation.2 | async-start | bytes 17039360 | tf_op jit(solution)/shard_map/all_gather | solution.py:116
  63.1 3.9 %copy-start.1 = (bf16[4,128,4096]{2,1,0:T(8,128)(2,1)S(1)}, bf16[4,128,4096]{2,1,0:T(8,128)(2,1)}, u32[]{:S(2)}) copy-start(bf16[4,128,4096]{2,1,0:T(8,128)(2,1)} %all-gather.4.cloned.1.call-done) | copy-start | bytes 12582916
  286.7 2.6 copy-start.2
Sparse Core Ops, SparseCore 0:
  10.9 52.0 all-gather.3
  69.5 206.1 all-gather.5

commit v2 on v1

v2 whole, which is shorter than its diff:
```python
import functools

import jax
import jax.numpy as jnp
from jax import lax
from jax.experimental import pallas as pl
from jax.experimental.pallas import tpu as pltpu
from jax.sharding import PartitionSpec as P

MESH = pl.DeviceIdType.MESH
HEADS = 4
HW = 128
ROWS = 128
WIDTH = 4096
DOCS = 4
RING = 8
COLS = 4
SLOTS = 4
CHUNKS = 4
LINE = 64


def rope_tables(place):
    positions = place * ROWS + jnp.arange(ROWS, dtype=jnp.int32)
    inverse = jnp.power(jnp.float32(500000.0), -jnp.arange(0, HW, 2, dtype=jnp.float32) / HW)
    angles = positions.astype(jnp.float32)[:, None] * inverse[None, :]
    cosine, sine = jnp.cos(angles), jnp.sin(angles)
    return jnp.concatenate([cosine, cosine], axis=1), jnp.concatenate([-sine, sine], axis=1)


def take(refs, *counts):
    refs = list(refs)
    out = []
    for count in counts:
        out.append(refs[:count] if count > 1 else refs[0])
        del refs[:count]
    return out


def kernel(vert_ref, slash_ref, tok_hbm, gain_ref, wq_hbm, wk_hbm, wv_hbm, cos_ref, sin_ref, out_hbm, *scratch):
    (
        tok, normed, w, kv, prev, ya, yb, xc, vy, vx, vz, qb, kall, vall, ob,
        local_sem, t_send, t_recv, f_send, f_recv, p_send, p_recv, z_send, z_recv, y_send, y_recv,
        x_send, x_recv, vy_send, vy_recv, vx_send, vx_recv, vz_send, vz_recv, o_send, o_recv,
    ) = take(
        scratch, 4, 4, 1, 4, 4, 4, 4, 4, 4, 4, 4, 4, 1, 1, 4, *([1] * 21)
    )
    s = lax.axis_index("seq")
    g = lax.axis_index("doc")
    z = lax.rem(s, RING)
    row = s // RING
    y = lax.rem(row, COLS)
    x = row // COLS
    docs = [g, g + 1 - 2 * lax.rem(g, 2), lax.rem(g + 2, 4), 3 - g]

    def at(seq, doc):
        return {"seq": seq, "doc": doc}

    z_up = at(s - z + lax.rem(z + 1, RING), g)
    z_down = at(s - z + lax.rem(z + RING - 1, RING), g)
    y_up = at(s - y * RING + lax.rem(y + 1, COLS) * RING, g)
    y_far = at(s - y * RING + lax.rem(y + 2, COLS) * RING, g)
    y_down = at(s - y * RING + lax.rem(y + 3, COLS) * RING, g)
    x_far = at(lax.rem(s + LINE // 2, LINE), g)
    after = at(lax.rem(s + 1, LINE), g)
    before = at(lax.rem(s + LINE - 1, LINE), g)
    mates = [None] + [at(s, docs[k]) for k in range(1, 4)]

    def remote(src, dst, send, recv, device):
        return pltpu.make_async_remote_copy(
            src_ref=src, dst_ref=dst, send_sem=send, recv_sem=recv, device_id=device, device_id_type=MESH
        )

    loads = [
        pltpu.make_async_copy(tok_hbm, tok[0], local_sem.at[0]),
        pltpu.make_async_copy(wk_hbm, w.at[:, 0:HW], local_sem.at[1]),
        pltpu.make_async_copy(wv_hbm, w.at[:, HW : 2 * HW], local_sem.at[2]),
        pltpu.make_async_copy(wq_hbm, w.at[:, 2 * HW :], local_sem.at[3]),
    ]
    for load in loads:
        load.start()

    barrier = pltpu.get_barrier_semaphore()
    greeted = mates[1:] + [z_up, z_down, y_up, y_far, y_down, x_far, after, before]
    for device in greeted:
        pl.semaphore_signal(barrier, inc=1, device_id=device, device_id_type=MESH)
    pl.semaphore_wait(barrier, len(greeted))

    part = ROWS // CHUNKS

    def rows_of(c):
        return pl.ds(c * part, part)

    across = [
        remote(tok_hbm.at[rows_of(c)], tok[2].at[rows_of(c)], t_send.at[c], t_recv.at[c], mates[2])
        for c in range(CHUNKS)
    ]
    beside = remote(tok_hbm, tok[1], t_send.at[CHUNKS], t_recv.at[CHUNKS], mates[1])
    onward = [
        remote(tok[2].at[rows_of(c)], tok[3].at[rows_of(c)], f_send.at[c], f_recv.at[c], mates[1])
        for c in range(CHUNKS)
    ]
    for copy in across:
        copy.start()
    beside.start()

    def norm(k, start, count):
        def body(i, carry):
            at_rows = pl.ds(pl.multiple_of(start + i * 16, 16), 16)
            wide = tok[k][at_rows, :].astype(jnp.float32)
            scale = lax.rsqrt(jnp.sum(wide * wide, axis=-1, keepdims=True) * (1.0 / WIDTH) + 1e-05)
            normed[k][at_rows, :] = (wide * scale * gain_ref[...]).astype(jnp.bfloat16)
            return carry

        lax.fori_loop(0, count // 16, body, 0)

    def rotate(value):
        return value * cos_ref[...] + pltpu.roll(value, HW // 2, 1) * sin_ref[...]

    def key_value(k):
        both = jnp.dot(normed[k][...], w[:, 0 : 2 * HW], preferred_element_type=jnp.float32)
        kv[k][z, :, 0:HW] = rotate(both[:, 0:HW]).astype(jnp.bfloat16)
        kv[k][z, :, HW:] = both[:, HW:].astype(jnp.bfloat16)

    def queries(k):
        wide = jnp.dot(normed[k][...], w[:, 2 * HW :], preferred_element_type=jnp.float32)
        for h in range(HEADS):
            qb[k][h * ROWS : (h + 1) * ROWS, :] = rotate(wide[:, h * HW : (h + 1) * HW]).astype(jnp.bfloat16)

    def ring(buf, k, send, recv, up, j):
        place = lax.rem(z - (j - 1) + RING, RING) if up else lax.rem(z + (j - 1), RING)
        index = (k * 2 + (0 if up else 1)) * 4 + j - 1
        return remote(buf.at[place], buf.at[place], send.at[index], recv.at[index], z_up if up else z_down)

    def ring_hops(k):
        return [(up, j) for j in range(1, 5) for up in (True, False) if j < 4 or up == (k % 2 == 0)]

    def ring_step(buf, k, send, recv, j):
        for up, hop in ring_hops(k):
            if hop == j - 1:
                ring(buf, k, send, recv, up, hop).wait_recv()
            if hop == j:
                ring(buf, k, send, recv, up, hop).start()

    def z_step(k, j):
        ring_step(kv[k], k, z_send, z_recv, j)

    def vz_step(k, j):
        ring_step(vz[k], k, vz_send, vz_recv, j)

    def prev_copy(k):
        return remote(kv[k].at[z], prev[k], p_send.at[k], p_recv.at[k], after)

    gives_prev = jnp.logical_and(z == RING - 1, s < LINE - 1)
    takes_prev = jnp.logical_and(z == 0, s > 0)

    def prev_start(k):
        @pl.when(gives_prev)
        def _():
            prev_copy(k).start()

    def prev_wait(k):
        @pl.when(takes_prev)
        def _():
            prev_copy(k).wait_recv()

    def offset(k, t):
        return slash_ref[docs[k] * 16 + g * 4 + t]

    def vertical(k, i):
        return vert_ref[docs[k] * 16 + g * 4 + i]

    def shift(k, t):
        return (offset(k, t) - z + RING - 1) // RING

    def turns(k, t):
        steps = lax.rem(shift(k, t), COLS)
        return steps if t < 2 else lax.rem(COLS - steps, COLS)

    def y_copies(k):
        return [
            remote(ya[k].at[0, 0:2], ya[k].at[1, 0:2], y_send.at[k * 3], y_recv.at[k * 3], y_up),
            remote(ya[k].at[0, 2:4], ya[k].at[1, 2:4], y_send.at[k * 3 + 1], y_recv.at[k * 3 + 1], y_down),
        ]

    def y_second(k):
        return remote(yb[k].at[0], yb[k].at[1], y_send.at[k * 3 + 2], y_recv.at[k * 3 + 2], y_far)

    def y_one(k):
        for t in range(SLOTS):
            ya[k][0, t] = kv[k][lax.rem(z - offset(k, t) + LINE, RING)]
        for copy in y_copies(k):
            copy.start()

    def y_two(k):
        for copy in y_copies(k):
            copy.wait_recv()
        for t in range(SLOTS):
            yb[k][0, t] = ya[k][lax.rem(turns(k, t), 2), t]
        y_second(k).start()

    def x_copy(k):
        return remote(xc[k].at[0], xc[k].at[1], x_send.at[k], x_recv.at[k], x_far)

    def x_one(k):
        y_second(k).wait_recv()
        for t in range(SLOTS):
            xc[k][0, t] = yb[k][turns(k, t) // 2, t]

        @pl.when(x == 0)
        def _():
            x_copy(k).start()

    def x_two(k):
        @pl.when(x == 1)
        def _():
            x_copy(k).wait_recv()

    def vy_copies(k):
        return [
            remote(vy[k].at[y], vy[k].at[y], vy_send.at[k * 3 + i], vy_recv.at[k * 3 + i], device)
            for i, device in enumerate((y_up, y_far, y_down))
        ]

    my_vertical = [vertical(k, lax.rem(z, 4)) for k in range(4)]

    def v_one(k):
        start = pl.multiple_of((z // 4) * 64, 64)
        vy[k][y] = kv[k][lax.rem(my_vertical[k], RING), pl.ds(start, 64), :]
        for copy in vy_copies(k):
            copy.start()

    def vx_copy(k):
        return remote(vx[k].at[0], vx[k].at[1], vx_send.at[k], vx_recv.at[k], x_far)

    def v_two(k):
        for copy in vy_copies(k):
            copy.wait_recv()
        vx[k][0] = vy[k][lax.rem(my_vertical[k] // RING, COLS)]

        @pl.when(x == 0)
        def _():
            vx_copy(k).start()

    def v_three(k):
        @pl.when(x == 1)
        def _():
            vx_copy(k).wait_recv()

        vz[k][z] = vx[k][x * (my_vertical[k] < LINE // 2).astype(jnp.int32)]
        vz_step(k, 1)

    def out_copy(k):
        columns = pl.ds(pl.multiple_of(g * 512, 512), 512)
        if k == 0:
            return pltpu.make_async_copy(ob[0], out_hbm.at[:, columns], local_sem.at[4])
        return remote(ob[k], out_hbm.at[:, columns], o_send.at[k], o_recv.at[k], mates[k])

    low = jnp.float32(-jnp.inf)

    def attend(k):
        def put(i, value):
            kall[i * ROWS : (i + 1) * ROWS, :] = value[:, 0:HW]
            vall[i * ROWS : (i + 1) * ROWS, :] = value[:, HW:]

        put(0, kv[k][z])

        @pl.when(z > 0)
        def _():
            put(1, kv[k][lax.rem(z + RING - 1, RING)])

        @pl.when(takes_prev)
        def _():
            put(1, prev[k][...])

        @pl.when(s == 0)
        def _():
            put(1, jnp.zeros((ROWS, 2 * HW), jnp.bfloat16))

        bias = [jnp.float32(0.0), jnp.where(s >= 1, jnp.float32(0.0), low)]
        for t in range(SLOTS):
            other = x * (shift(k, t) > y).astype(jnp.int32)
            put(2 + t, xc[k][other, t])
            bias.append(jnp.where(s >= offset(k, t), jnp.float32(0.0), low))
        for i in range(4):
            at_block = (2 + SLOTS + i) * ROWS
            for half in range(2):
                value = vz[k][i + 4 * half]
                kall[at_block + half * 64 : at_block + half * 64 + 64, :] = value[:, 0:HW]
                vall[at_block + half * 64 : at_block + half * 64 + 64, :] = value[:, HW:]
            block = vertical(k, i)
            good = block < s - 1
            for t in range(SLOTS):
                good = jnp.logical_and(good, block != s - offset(k, t))
            bias.append(jnp.where(good, jnp.float32(0.0), low))
        blocks = len(bias)
        causal = lax.broadcasted_iota(jnp.int32, (ROWS, ROWS), 1) <= lax.broadcasted_iota(jnp.int32, (ROWS, ROWS), 0)

        def head(h, carry):
            query = qb[k][pl.ds(pl.multiple_of(h * ROWS, ROWS), ROWS), :]
            scores = lax.dot_general(
                query, kall[...], (((1,), (1,)), ((), ())), preferred_element_type=jnp.float32
            ) * (HW ** (-0.5))
            tiles = [scores[:, i * ROWS : (i + 1) * ROWS] for i in range(blocks)]
            tiles = [jnp.where(causal, tiles[0], low)] + [tiles[i] + bias[i] for i in range(1, blocks)]
            highest = tiles[0]
            for tile in tiles[1:]:
                highest = jnp.maximum(highest, tile)
            highest = jnp.max(highest, axis=1, keepdims=True)
            raised = [jnp.exp(tile - highest) for tile in tiles]
            total = raised[0]
            for tile in raised[1:]:
                total = total + tile
            total = jnp.sum(total, axis=1, keepdims=True)
            weights = jnp.concatenate([tile.astype(jnp.bfloat16) for tile in raised], axis=1)
            mixed = jnp.dot(weights, vall[...], preferred_element_type=jnp.float32) / total
            ob[k][:, pl.ds(pl.multiple_of(h * HW, HW), HW)] = mixed.astype(jnp.bfloat16)
            return carry

        lax.fori_loop(0, HEADS, head, 0)
        out_copy(k).start()

    def arrive(c):
        across[c].wait_recv()
        onward[c].start()
        norm(2, c * part, part)

    loads[0].wait()
    norm(0, 0, ROWS)
    loads[1].wait()
    loads[2].wait()
    key_value(0)
    z_step(0, 1)
    prev_start(0)
    beside.wait_recv()
    norm(1, 0, ROWS)
    key_value(1)
    z_step(1, 1)
    prev_start(1)
    loads[3].wait()
    queries(0)
    z_step(0, 2)
    z_step(1, 2)
    arrive(0)
    queries(1)
    z_step(0, 3)
    z_step(1, 3)
    z_step(0, 4)
    z_step(1, 4)
    arrive(1)
    z_step(0, 5)
    y_one(0)
    v_one(0)
    z_step(1, 5)
    y_one(1)
    v_one(1)
    arrive(2)
    y_two(0)
    y_two(1)
    v_two(0)
    v_two(1)
    arrive(3)
    key_value(2)
    z_step(2, 1)
    prev_start(2)
    for copy in onward:
        copy.wait_recv()
    norm(3, 0, ROWS)
    key_value(3)
    z_step(3, 1)
    prev_start(3)
    x_one(0)
    v_three(0)
    z_step(2, 2)
    x_one(1)
    v_three(1)
    z_step(3, 2)
    queries(2)
    z_step(2, 3)
    z_step(3, 3)
    vz_step(0, 2)
    vz_step(1, 2)
    queries(3)
    z_step(2, 4)
    z_step(3, 4)
    vz_step(0, 3)
    vz_step(1, 3)
    z_step(2, 5)
    y_one(2)
    v_one(2)
    z_step(3, 5)
    y_one(3)
    v_one(3)
    for j in (4, 5):
        vz_step(0, j)
        vz_step(1, j)
    prev_wait(0)
    x_two(0)
    attend(0)
    y_two(2)
    v_two(2)
    y_two(3)
    v_two(3)
    prev_wait(1)
    x_two(1)
    attend(1)
    x_one(2)
    v_three(2)
    x_one(3)
    v_three(3)
    for j in (2, 3, 4, 5):
        vz_step(2, j)
        vz_step(3, j)
    prev_wait(2)
    x_two(2)
    attend(2)
    prev_wait(3)
    x_two(3)
    attend(3)

    for copy in across + [beside] + onward:
        copy.wait_send()
    for k in range(4):
        for up, j in ring_hops(k):
            ring(kv[k], k, z_send, z_recv, up, j).wait_send()
            ring(vz[k], k, vz_send, vz_recv, up, j).wait_send()
        for copy in y_copies(k) + [y_second(k)] + vy_copies(k):
            copy.wait_send()

        @pl.when(gives_prev)
        def _():
            prev_copy(k).wait_send()

        @pl.when(x == 0)
        def _():
            x_copy(k).wait_send()
            vx_copy(k).wait_send()

    for k in range(4):
        out_copy(k).wait()


def local(tokens, norm_gain, w_query, key_weight, value_weight, vertical_blocks, slash_offsets):
    cosine, sine = rope_tables(lax.axis_index("seq"))
    bf16 = jnp.bfloat16
    unit = (ROWS, 2 * HW)
    dma = pltpu.SemaphoreType.DMA

    def many(shape):
        return [pltpu.VMEM(shape, bf16)] * DOCS

    scratch = (
        many((ROWS, WIDTH))
        + many((ROWS, WIDTH))
        + [pltpu.VMEM((WIDTH, 6 * HW), bf16)]
        + many((RING,) + unit)
        + many(unit)
        + many((2, SLOTS) + unit)
        + many((2, SLOTS) + unit)
        + many((2, SLOTS) + unit)
        + many((COLS, 64, 2 * HW))
        + many((2, 64, 2 * HW))
        + many((RING, 64, 2 * HW))
        + many((HEADS * ROWS, HW))
        + [pltpu.VMEM((10 * ROWS, HW), bf16)] * 2
        + many((ROWS, HEADS * HW))
        + [dma((5,))]
        + [dma((CHUNKS + 1,))] * 2
        + [dma((CHUNKS,))] * 2
        + [dma((4,))] * 2
        + [dma((32,))] * 2
        + [dma((12,))] * 2
        + [dma((4,))] * 2
        + [dma((12,))] * 2
        + [dma((4,))] * 2
        + [dma((32,))] * 2
        + [dma((4,))] * 2
    )
    smem = pl.BlockSpec(memory_space=pltpu.SMEM)
    vmem = pl.BlockSpec(memory_space=pltpu.VMEM)
    hbm = pl.BlockSpec(memory_space=pl.ANY)
    out = pl.pallas_call(
        kernel,
        out_shape=jax.ShapeDtypeStruct((ROWS, DOCS * HEADS * HW), bf16),
        in_specs=[smem, smem, hbm, vmem, hbm, hbm, hbm, vmem, vmem],
        out_specs=hbm,
        scratch_shapes=scratch,
        compiler_params=pltpu.CompilerParams(
            collective_id=0, has_side_effects=True, vmem_limit_bytes=60 * 1024 * 1024
        ),
    )(
        vertical_blocks.reshape(-1),
        slash_offsets.reshape(-1),
        tokens[0],
        norm_gain[None, :],
        w_query,
        key_weight,
        value_weight,
        cosine,
        sine,
    )
    return out[None]


def solution(mesh):
    return jax.shard_map(
        local,
        mesh=mesh,
        in_specs=(
            P("doc", "seq", None),
            P(),
            P(None, "doc"),
            P(None, "doc"),
            P(None, "doc"),
            P(),
            P(),
        ),
        out_specs=P("doc", "seq", None),
        check_vma=False,
    )
```

time: 315 us -> 127 us (0.40)
  the two profiles are of different devices: /device:TPU:5 before, /device:TPU:31 now
where the time goes in v2:
time: 127 us
  Pallas kernels  121 us (95%)
  local copies, waits for them, and re-layouts  4.54 us (4%)
    pallas_call x1, Pallas kernels, local(): pl.pallas_call(kernel, out_shape=jax.ShapeDtypeStruct((ROWS, DOCS * HEADS...  121 us

profile of v2, /device:TPU:31, one launch (start us, length us, event | category | flops | bytes accessed | tf_op | source)
XLA Modules:
  0.0 126.6 jit_solution(12742640424206814263)
XLA Ops:
  0.0 1.4 %reshape.18.vert_ref = s32[64]{0:T(128)} reshape(s32[4,4,4]{2,1,0:T(4,128)} %param.12) | data formatting | bytes 512 | tf_op jit(solution)/shard_map/reshape | solution.py:492
  1.4 1.3 %reshape.19.slash_ref = s32[64]{0:T(128)} reshape(s32[4,4,4]{2,1,0:T(4,128)} %param.13) | data formatting | bytes 512 | tf_op jit(solution)/shard_map/reshape | solution.py:493
  2.7 0.3 fusion
  3.0 0.7 pad_maximum_fusion
  3.7 121.0 %shard_map.73 = bf16[128,2048]{1,0:T(8,128)(2,1)} custom-call(s32[64]{0:T(128)} %reshape.18.vert_ref, s32[64]{0:T(128)} %reshape.19.slash_ref, bf16[128,4096]{1,0:T(8,128)(2,1)} %bitcast.4, f32[1,4096]{1,0:T(1,128)} %bitcast.5, bf16[4096,512]{1,0:T(8,128)(2,1)} %wq_hbm.1, bf16[4096,128]{1,0:T(8,128)(2,1)} %wk_hbm.1, bf16[4096,128]{1,0:T(8,128)(2,1)} %wv_hbm.1, ...), custom_call_target="tpu_custom_call" | custom-call | tf_op jit(solution)/shard_map/pallas_call | solution.py:482
  124.7 1.9 %copy.9 = bf16[1,128,2048]{2,1,0:T(8,128)(2,1)} copy(bf16[1,128,2048]{2,1,0:T(8,128)(2,1)} %bitcast.3) | data formatting | bytes 1048576
  (2 shorter events, 0.0 us)

commit v3 on v2

v3 whole, which is shorter than its diff:
```python
import functools

import jax
import jax.numpy as jnp
from jax import lax
from jax.experimental import pallas as pl
from jax.experimental.pallas import tpu as pltpu
from jax.sharding import PartitionSpec as P

MESH = pl.DeviceIdType.MESH
HEADS = 4
HW = 128
ROWS = 128
WIDTH = 4096
DOCS = 4
RING = 8
COLS = 4
SLOTS = 4
CHUNKS = 4
PART = ROWS // CHUNKS
LINE = 64

PLAN = [
    ("own", 0), ("kv", 0), ("z", 0, 1), ("prev", 0),
    ("beside", 1), ("kv", 1), ("z", 1, 1), ("prev", 1),
    ("arrive", 2, 0), ("z", 0, 2), ("z", 1, 2), ("q", 0),
    ("arrive", 2, 1), ("z", 0, 3), ("z", 1, 3),
    ("arrive", 2, 2), ("z", 0, 4), ("z", 1, 4), ("q", 1),
    ("arrive", 2, 3), ("kv", 2), ("z", 2, 1), ("prev", 2),
    ("z", 0, 5), ("y1", 0), ("v1", 0), ("z", 1, 5), ("y1", 1), ("v1", 1), ("z", 2, 2),
    ("arrive", 3, 0), ("z", 2, 3), ("y2", 0), ("v2", 0),
    ("arrive", 3, 1), ("z", 2, 4), ("y2", 1), ("v2", 1), ("q", 2), ("z", 2, 5), ("y1", 2), ("v1", 2),
    ("arrive", 3, 2),
    ("arrive", 3, 3), ("kv", 3), ("z", 3, 1), ("prev", 3),
    ("x1", 0), ("v3", 0), ("x1", 1), ("v3", 1), ("z", 3, 2), ("y2", 2), ("v2", 2),
    ("vz", 0, 2), ("vz", 1, 2), ("z", 3, 3), ("vz", 0, 3), ("vz", 1, 3), ("q", 3),
    ("z", 3, 4), ("x1", 2), ("v3", 2), ("z", 3, 5), ("y1", 3), ("v1", 3),
    ("vz", 0, 4), ("vz", 1, 4), ("vz", 0, 5), ("vz", 1, 5), ("attend", 0),
    ("y2", 3), ("v2", 3), ("vz", 2, 2), ("attend", 1), ("vz", 2, 3), ("x1", 3), ("v3", 3),
    ("vz", 2, 4), ("vz", 2, 5), ("vz", 3, 2), ("attend", 2),
    ("vz", 3, 3), ("vz", 3, 4), ("vz", 3, 5), ("attend", 3),
]


def rope_tables(place):
    positions = place * ROWS + jnp.arange(ROWS, dtype=jnp.int32)
    inverse = jnp.power(jnp.float32(500000.0), -jnp.arange(0, HW, 2, dtype=jnp.float32) / HW)
    angles = positions.astype(jnp.float32)[:, None] * inverse[None, :]
    cosine, sine = jnp.cos(angles), jnp.sin(angles)
    return jnp.concatenate([cosine, cosine], axis=1), jnp.concatenate([-sine, sine], axis=1)


def take(refs, *counts):
    refs = list(refs)
    out = []
    for count in counts:
        out.append(refs[:count] if count > 1 else refs[0])
        del refs[:count]
    return out


def guarded(condition, act):
    if condition is None:
        act()
    else:
        pl.when(condition)(act)


class Copy:
    def __init__(self, log, src, dst, send, recv, device, sends=None, takes=None):
        self.log, self.parts = log, (src, dst, send, recv, device)
        self.sends, self.takes = sends, takes
        self.landed = False

    def make(self):
        src, dst, send, recv, device = self.parts
        return pltpu.make_async_remote_copy(
            src_ref=src, dst_ref=dst, send_sem=send, recv_sem=recv, device_id=device, device_id_type=MESH
        )

    def start(self):
        guarded(self.sends, lambda: self.make().start())
        self.log.append(self)

    def land(self):
        guarded(self.takes, lambda: self.make().wait_recv())
        self.landed = True

    def sent(self):
        guarded(self.sends, lambda: self.make().wait_send())


def kernel(plan, vert_ref, slash_ref, tok_hbm, gain_ref, wq_hbm, wk_hbm, wv_hbm, cos_ref, sin_ref, out_hbm, *scratch):
    (
        tok, normed, w, kv, prev, ya, yb, xc, vy, vx, vz, qb, kall, vall, ob,
        local_sem, t_send, t_recv, f_send, p_send, p_recv, z_send, z_recv, y_send, y_recv,
        x_send, x_recv, vy_send, vy_recv, vx_send, vx_recv, vz_send, vz_recv, o_send, o_recv,
    ) = take(scratch, 4, 4, 1, 4, 4, 4, 4, 4, 4, 4, 4, 4, 1, 1, 4, *([1] * 20))
    s = lax.axis_index("seq")
    g = lax.axis_index("doc")
    core = lax.rem(g, 2)
    z = lax.rem(s, RING)
    row = s // RING
    y = lax.rem(row, COLS)
    x = row // COLS
    across = lax.rem(g - core + 2, 4)
    docs = [g, g + 1 - 2 * core, across, across + 1]

    def at(seq, doc):
        return {"seq": seq, "doc": doc}

    z_up = at(s - z + lax.rem(z + 1, RING), g)
    z_down = at(s - z + lax.rem(z + RING - 1, RING), g)
    y_up = at(s - y * RING + lax.rem(y + 1, COLS) * RING, g)
    y_far = at(s - y * RING + lax.rem(y + 2, COLS) * RING, g)
    y_down = at(s - y * RING + lax.rem(y + 3, COLS) * RING, g)
    x_far = at(lax.rem(s + LINE // 2, LINE), g)
    after = at(lax.rem(s + 1, LINE), g)
    before = at(lax.rem(s + LINE - 1, LINE), g)
    mates = [at(s, doc) for doc in docs]
    peer = at(s, across + core)

    log = []

    def remote(*parts, **ends):
        return Copy(log, *parts, **ends)

    loads = [
        pltpu.make_async_copy(tok_hbm, tok[0], local_sem.at[0]),
        pltpu.make_async_copy(wk_hbm, w.at[:, 0:HW], local_sem.at[1]),
        pltpu.make_async_copy(wv_hbm, w.at[:, HW : 2 * HW], local_sem.at[2]),
        pltpu.make_async_copy(wq_hbm, w.at[:, 2 * HW :], local_sem.at[3]),
    ]
    for load in loads:
        load.start()

    barrier = pltpu.get_barrier_semaphore()
    greeted = mates[1:] + [z_up, z_down, y_up, y_far, y_down, x_far, after, before]
    for device in greeted:
        pl.semaphore_signal(barrier, inc=1, device_id=device, device_id_type=MESH)
    pl.semaphore_wait(barrier, len(greeted))

    even, odd = core == 0, core == 1
    lower, upper = x == 0, x == 1
    gives_prev = jnp.logical_and(z == RING - 1, s < LINE - 1)
    takes_prev = jnp.logical_and(z == 0, s > 0)

    def rows_of(c):
        return pl.ds(c * PART, PART)

    def chunk_sem(k, c):
        return t_recv.at[(k - 2) * CHUNKS + c]

    crossing = [
        [
            remote(
                tok_hbm.at[rows_of(c)], tok[k].at[rows_of(c)], t_send.at[c], chunk_sem(k, c), peer,
                sends=even if k == 2 else odd,
            )
            for c in range(CHUNKS)
        ]
        for k in (2, 3)
    ]
    handed = [
        [
            remote(
                tok[k].at[rows_of(c)], tok[k].at[rows_of(c)], f_send.at[c], chunk_sem(k, c), mates[1],
                sends=even if k == 2 else odd,
            )
            for c in range(CHUNKS)
        ]
        for k in (2, 3)
    ]
    beside = remote(tok_hbm, tok[1], t_send.at[CHUNKS], t_recv.at[2 * CHUNKS], mates[1])

    def norm(k, start, count):
        def body(i, carry):
            at_rows = pl.ds(pl.multiple_of(start + i * 16, 16), 16)
            wide = tok[k][at_rows, :].astype(jnp.float32)
            scale = lax.rsqrt(jnp.sum(wide * wide, axis=-1, keepdims=True) * (1.0 / WIDTH) + 1e-05)
            normed[k][at_rows, :] = (wide * scale * gain_ref[...]).astype(jnp.bfloat16)
            return carry

        lax.fori_loop(0, count // 16, body, 0)

    def do_own(k):
        loads[0].wait()
        norm(0, 0, ROWS)

    def do_beside(k):
        beside.land()
        norm(1, 0, ROWS)

    def do_arrive(k, c):
        crossing[k - 2][c].land()
        handed[k - 2][c].start()
        handed[k - 2][c].landed = True
        if k == 2 and c == CHUNKS - 2:
            for copy in crossing[1]:
                copy.start()
        norm(k, c * PART, PART)

    def rotate(value):
        return value * cos_ref[...] + pltpu.roll(value, HW // 2, 1) * sin_ref[...]

    ready = set()

    def loaded(*which):
        for i in which:
            if i not in ready:
                loads[i].wait()
                ready.add(i)

    def do_kv(k):
        loaded(1, 2)
        both = jnp.dot(normed[k][...], w[:, 0 : 2 * HW], preferred_element_type=jnp.float32)
        kv[k][z, :, 0:HW] = rotate(both[:, 0:HW]).astype(jnp.bfloat16)
        kv[k][z, :, HW:] = both[:, HW:].astype(jnp.bfloat16)

    def do_q(k):
        loaded(3)
        wide = jnp.dot(normed[k][...], w[:, 2 * HW :], preferred_element_type=jnp.float32)
        for h in range(HEADS):
            qb[k][h * ROWS : (h + 1) * ROWS, :] = rotate(wide[:, h * HW : (h + 1) * HW]).astype(jnp.bfloat16)

    def ring(buf, k, send, recv):
        hops = {}
        for j in range(1, 5):
            for up in (True, False):
                if j == 4 and up != (k % 2 == 0):
                    continue
                place = lax.rem(z - (j - 1) + RING, RING) if up else lax.rem(z + (j - 1), RING)
                index = (k * 2 + (0 if up else 1)) * 4 + j - 1
                hops[up, j] = remote(
                    buf.at[place], buf.at[place], send.at[index], recv.at[index], z_up if up else z_down
                )
        return hops

    z_hops = [ring(kv[k], k, z_send, z_recv) for k in range(DOCS)]
    vz_hops = [ring(vz[k], k, vz_send, vz_recv) for k in range(DOCS)]

    def step(hops, j):
        for up in (True, False):
            if (up, j - 1) in hops:
                hops[up, j - 1].land()
            if (up, j) in hops:
                hops[up, j].start()

    def do_z(k, j):
        step(z_hops[k], j)

    def do_vz(k, j):
        step(vz_hops[k], j)

    prevs = [
        remote(kv[k].at[z], prev[k], p_send.at[k], p_recv.at[k], after, sends=gives_prev, takes=takes_prev)
        for k in range(DOCS)
    ]

    def do_prev(k):
        prevs[k].start()

    offset = [[slash_ref[docs[k], g, t] for t in range(SLOTS)] for k in range(DOCS)]
    vertical = [[vert_ref[docs[k], g, i] for i in range(4)] for k in range(DOCS)]
    mine = [vert_ref[docs[k], g, lax.rem(z, 4)] for k in range(DOCS)]
    shift = [[(offset[k][t] - z + RING - 1) // RING for t in range(SLOTS)] for k in range(DOCS)]

    def turns(k, t):
        steps = lax.rem(shift[k][t], COLS)
        return steps if t < 2 else lax.rem(COLS - steps, COLS)

    y_near = [
        [
            remote(ya[k].at[0, 0:2], ya[k].at[1, 0:2], y_send.at[k * 3], y_recv.at[k * 3], y_up),
            remote(ya[k].at[0, 2:4], ya[k].at[1, 2:4], y_send.at[k * 3 + 1], y_recv.at[k * 3 + 1], y_down),
        ]
        for k in range(DOCS)
    ]
    y_over = [
        remote(yb[k].at[0], yb[k].at[1], y_send.at[k * 3 + 2], y_recv.at[k * 3 + 2], y_far) for k in range(DOCS)
    ]
    x_over = [
        remote(xc[k].at[0], xc[k].at[1], x_send.at[k], x_recv.at[k], x_far, sends=lower, takes=upper)
        for k in range(DOCS)
    ]
    vy_over = [
        [
            remote(vy[k].at[y], vy[k].at[y], vy_send.at[k * 3 + i], vy_recv.at[k * 3 + i], device)
            for i, device in enumerate((y_up, y_far, y_down))
        ]
        for k in range(DOCS)
    ]
    vx_over = [
        remote(vx[k].at[0], vx[k].at[1], vx_send.at[k], vx_recv.at[k], x_far, sends=lower, takes=upper)
        for k in range(DOCS)
    ]

    def do_y1(k):
        for t in range(SLOTS):
            ya[k][0, t] = kv[k][lax.rem(z - offset[k][t] + LINE, RING)]
        for copy in y_near[k]:
            copy.start()

    def do_y2(k):
        for copy in y_near[k]:
            copy.land()
        for t in range(SLOTS):
            yb[k][0, t] = ya[k][lax.rem(turns(k, t), 2), t]
        y_over[k].start()

    def do_x1(k):
        y_over[k].land()
        for t in range(SLOTS):
            xc[k][0, t] = yb[k][turns(k, t) // 2, t]
        x_over[k].start()

    def do_v1(k):
        start = pl.multiple_of((z // 4) * 64, 64)
        vy[k][y] = kv[k][lax.rem(mine[k], RING), pl.ds(start, 64), :]
        for copy in vy_over[k]:
            copy.start()

    def do_v2(k):
        for copy in vy_over[k]:
            copy.land()
        vx[k][0] = vy[k][lax.rem(mine[k] // RING, COLS)]
        vx_over[k].start()

    def do_v3(k):
        vx_over[k].land()
        vz[k][z] = vx[k][x * (mine[k] < LINE // 2).astype(jnp.int32)]
        do_vz(k, 1)

    columns = pl.ds(pl.multiple_of(g * 512, 512), 512)
    out_own = pltpu.make_async_copy(ob[0], out_hbm.at[:, columns], local_sem.at[4])
    out_sent = [None] + [
        remote(ob[k], out_hbm.at[:, columns], o_send.at[k], o_recv.at[0 if k == 1 else 1 + core], mates[k])
        for k in range(1, DOCS)
    ]
    out_got = [remote(ob[1], out_hbm.at[:, columns], o_send.at[1], o_recv.at[i], mates[1]) for i in range(3)]

    low = jnp.float32(-jnp.inf)

    def do_attend(k):
        prevs[k].land()
        x_over[k].land()

        def put(i, value):
            kall[i * ROWS : (i + 1) * ROWS, :] = value[:, 0:HW]
            vall[i * ROWS : (i + 1) * ROWS, :] = value[:, HW:]

        put(0, kv[k][z])

        @pl.when(z > 0)
        def _():
            put(1, kv[k][lax.rem(z + RING - 1, RING)])

        @pl.when(takes_prev)
        def _():
            put(1, prev[k][...])

        @pl.when(s == 0)
        def _():
            put(1, jnp.zeros((ROWS, 2 * HW), jnp.bfloat16))

        bias = [jnp.float32(0.0), jnp.where(s >= 1, jnp.float32(0.0), low)]
        for t in range(SLOTS):
            other = x * (shift[k][t] > y).astype(jnp.int32)
            put(2 + t, xc[k][other, t])
            bias.append(jnp.where(s >= offset[k][t], jnp.float32(0.0), low))
        for i in range(4):
            at_block = (2 + SLOTS + i) * ROWS
            for half in range(2):
                value = vz[k][i + 4 * half]
                kall[at_block + half * 64 : at_block + half * 64 + 64, :] = value[:, 0:HW]
                vall[at_block + half * 64 : at_block + half * 64 + 64, :] = value[:, HW:]
            block = vertical[k][i]
            good = block < s - 1
            for t in range(SLOTS):
                good = jnp.logical_and(good, block != s - offset[k][t])
            bias.append(jnp.where(good, jnp.float32(0.0), low))
        blocks = len(bias)
        causal = lax.broadcasted_iota(jnp.int32, (ROWS, ROWS), 1) <= lax.broadcasted_iota(jnp.int32, (ROWS, ROWS), 0)

        def head(h, carry):
            query = qb[k][pl.ds(pl.multiple_of(h * ROWS, ROWS), ROWS), :]
            scores = lax.dot_general(
                query, kall[...], (((1,), (1,)), ((), ())), preferred_element_type=jnp.float32
            ) * (HW ** (-0.5))
            tiles = [scores[:, i * ROWS : (i + 1) * ROWS] for i in range(blocks)]
            tiles = [jnp.where(causal, tiles[0], low)] + [tiles[i] + bias[i] for i in range(1, blocks)]
            highest = tiles[0]
            for tile in tiles[1:]:
                highest = jnp.maximum(highest, tile)
            highest = jnp.max(highest, axis=1, keepdims=True)
            raised = [jnp.exp(tile - highest) for tile in tiles]
            total = raised[0]
            for tile in raised[1:]:
                total = total + tile
            total = jnp.sum(total, axis=1, keepdims=True)
            weights = jnp.concatenate([tile.astype(jnp.bfloat16) for tile in raised], axis=1)
            mixed = jnp.dot(weights, vall[...], preferred_element_type=jnp.float32) / total
            ob[k][:, pl.ds(pl.multiple_of(h * HW, HW), HW)] = mixed.astype(jnp.bfloat16)
            return carry

        lax.fori_loop(0, HEADS, head, 0)
        if k == 0:
            out_own.start()
        else:
            out_sent[k].start()
            out_sent[k].landed = True

    for copy in crossing[0]:
        copy.start()
    beside.start()
    does = {
        "own": do_own, "beside": do_beside, "arrive": do_arrive, "kv": do_kv, "q": do_q, "z": do_z, "vz": do_vz,
        "prev": do_prev, "y1": do_y1, "y2": do_y2, "x1": do_x1, "v1": do_v1, "v2": do_v2, "v3": do_v3,
        "attend": do_attend,
    }
    for name, *which in plan:
        does[name](*which)

    loaded(1, 2, 3)
    for copy in log:
        if not copy.landed:
            copy.land()
        copy.sent()
    if ("attend", 0) in plan:
        out_own.wait()
    for i in range(3):
        if ("attend", i + 1) in plan:
            out_got[i].land()


def layer(plan, collective_id, tokens, norm_gain, w_query, key_weight, value_weight, vertical_blocks, slash_offsets):
    cosine, sine = rope_tables(lax.axis_index("seq"))
    bf16 = jnp.bfloat16
    unit = (ROWS, 2 * HW)
    dma = pltpu.SemaphoreType.DMA

    def many(shape):
        return [pltpu.VMEM(shape, bf16)] * DOCS

    scratch = (
        many((ROWS, WIDTH))
        + many((ROWS, WIDTH))
        + [pltpu.VMEM((WIDTH, 6 * HW), bf16)]
        + many((RING,) + unit)
        + many(unit)
        + many((2, SLOTS) + unit) * 3
        + many((COLS, 64, 2 * HW))
        + many((2, 64, 2 * HW))
        + many((RING, 64, 2 * HW))
        + many((HEADS * ROWS, HW))
        + [pltpu.VMEM((10 * ROWS, HW), bf16)] * 2
        + many((ROWS, HEADS * HW))
        + [dma((5,)), dma((CHUNKS + 1,)), dma((2 * CHUNKS + 1,)), dma((CHUNKS,))]
    )
    for count in (4, 32, 12, 4, 12, 4, 32, 4):
        scratch += [dma((count,))] * 2
    smem = pl.BlockSpec(memory_space=pltpu.SMEM)
    vmem = pl.BlockSpec(memory_space=pltpu.VMEM)
    hbm = pl.BlockSpec(memory_space=pl.ANY)
    out = pl.pallas_call(
        functools.partial(kernel, plan),
        out_shape=jax.ShapeDtypeStruct((ROWS, DOCS * HEADS * HW), bf16),
        in_specs=[smem, smem, hbm, vmem, hbm, hbm, hbm, vmem, vmem],
        out_specs=hbm,
        scratch_shapes=scratch,
        compiler_params=pltpu.CompilerParams(
            collective_id=collective_id, has_side_effects=True, vmem_limit_bytes=60 * 1024 * 1024
        ),
    )(
        vertical_blocks, slash_offsets, tokens[0], norm_gain[None, :], w_query, key_weight, value_weight, cosine, sine
    )
    return out[None]


IN_SPECS = (
    P("doc", "seq", None),
    P(),
    P(None, "doc"),
    P(None, "doc"),
    P(None, "doc"),
    P(),
    P(),
)


def solution(mesh):
    return jax.shard_map(
        functools.partial(layer, PLAN, 0),
        mesh=mesh,
        in_specs=IN_SPECS,
        out_specs=P("doc", "seq", None),
        check_vma=False,
    )
```

time: 127 us -> 111 us (0.87)
  the two profiles are of different devices: /device:TPU:31 before, /device:TPU:5 now
where the time goes in v3:
time: 111 us; the launch traced here: 110 us
  Pallas kernels  107 us (96%)
  local copies, waits for them, and re-layouts  1.88 us (2%)
    pallas_call x1, Pallas kernels, layer(): pl.pallas_call(functools.partial(kernel, plan), out_shape=jax.ShapeDtypeS...  107 us

profile of v3, /device:TPU:5, one launch (start us, length us, event | category | flops | bytes accessed | tf_op | source)
XLA Modules:
  0.0 110.0 jit_solution(845524003701215126)
XLA Ops:
  0.0 0.3 fusion
  0.3 0.7 pad_maximum_fusion
  1.1 107.1 %shard_map.73 = bf16[128,2048]{1,0:T(8,128)(2,1)} custom-call(s32[4,4,4]{2,1,0:T(4,128)} %vert_ref.1, s32[4,4,4]{2,1,0:T(4,128)} %slash_ref.1, bf16[128,4096]{1,0:T(8,128)(2,1)} %bitcast.4, f32[1,4096]{1,0:T(1,128)} %bitcast.5, bf16[4096,512]{1,0:T(8,128)(2,1)} %wq_hbm.1, bf16[4096,128]{1,0:T(8,128)(2,1)} %wk_hbm.1, bf16[4096,128]{1,0:T(8,128)(2,1)} %wv_hbm.1, ...), custom_call_target="tpu_custom_call" | custom-call | tf_op jit(solution)/shard_map/pallas_call | solution.py:465
  108.2 1.9 %copy.9 = bf16[1,128,2048]{2,1,0:T(8,128)(2,1)} copy(bf16[1,128,2048]{2,1,0:T(8,128)(2,1)} %bitcast.3) | data formatting | bytes 1048576
  (2 shorter events, 0.0 us)

commit v4 on v3

v4 whole, which is shorter than its diff:
```python
import functools

import jax
import jax.numpy as jnp
from jax import lax
from jax.experimental import pallas as pl
from jax.experimental.pallas import tpu as pltpu
from jax.sharding import PartitionSpec as P

MESH = pl.DeviceIdType.MESH
HEADS = 4
HW = 128
ROWS = 128
HALF = ROWS // 2
WIDTH = 4096
DOCS = 4
UNITS = 2 * DOCS
RING = 8
COLS = 4
SLOTS = 4
CHUNKS = 4
PART = ROWS // CHUNKS
LINE = 64

PLAN = [
    ("own", 0), ("kv", 0, 0), ("kv", 0, 1), ("z", 0, 0, 1), ("prev", 0, 0), ("z", 0, 1, 1), ("prev", 0, 1), ("q", 0),
    ("beside", 1), ("kv", 1, 0), ("arrive", 2, 0), ("kv", 1, 1), ("z", 1, 0, 1), ("prev", 1, 0), ("z", 1, 1, 1),
    ("prev", 1, 1), ("z", 0, 0, 2), ("z", 0, 1, 2), ("q", 1), ("arrive", 2, 1), ("kv", 2, 0), ("z", 2, 0, 1),
    ("prev", 2, 0), ("z", 1, 0, 2), ("z", 1, 1, 2), ("z", 0, 0, 3), ("z", 0, 1, 3), ("arrive", 2, 2), ("z", 2, 0, 2),
    ("z", 1, 0, 3), ("z", 1, 1, 3), ("z", 0, 0, 4), ("arrive", 2, 3), ("kv", 2, 1), ("z", 2, 1, 1), ("prev", 2, 1),
    ("z", 0, 1, 4), ("q", 2), ("z", 2, 0, 3), ("z", 1, 0, 4), ("z", 1, 1, 4), ("z", 0, 0, 5), ("y1", 0, 0),
    ("arrive", 3, 0), ("z", 0, 1, 5), ("z", 2, 1, 2), ("v1", 0), ("y1", 0, 1), ("z", 2, 0, 4), ("z", 1, 0, 5),
    ("z", 1, 1, 5), ("v1", 1), ("y1", 1, 0), ("y1", 1, 1), ("arrive", 3, 1), ("kv", 3, 0), ("z", 3, 0, 1),
    ("prev", 3, 0), ("z", 2, 1, 3), ("y2", 0, 0), ("z", 2, 0, 5), ("y1", 2, 0), ("arrive", 3, 2), ("y2", 0, 1),
    ("z", 3, 0, 2), ("z", 2, 1, 4), ("arrive", 3, 3), ("kv", 3, 1), ("z", 3, 0, 3), ("z", 3, 1, 1), ("prev", 3, 1),
    ("z", 2, 1, 5), ("v1", 2), ("y1", 2, 1), ("v2", 1), ("y2", 1, 0), ("v2", 0), ("q", 3), ("y2", 1, 1),
    ("z", 3, 0, 4), ("z", 3, 1, 2), ("v3", 1), ("v3", 0), ("x1", 0, 0), ("z", 3, 0, 5), ("y1", 3, 0), ("y2", 2, 0),
    ("z", 3, 1, 3), ("vz", 1, 2), ("vz", 0, 2), ("z", 3, 1, 4), ("vz", 1, 3), ("x1", 0, 1), ("vz", 0, 3), ("v2", 2),
    ("z", 3, 1, 5), ("v1", 3), ("y1", 3, 1), ("y2", 2, 1), ("vz", 1, 4), ("vz", 0, 4), ("vz", 1, 5), ("vz", 0, 5),
    ("stage", 0), ("x1", 1, 0), ("v3", 2), ("head", 0, 0), ("head", 0, 1), ("head", 0, 2), ("vz", 2, 2),
    ("x1", 1, 1), ("head", 0, 3), ("y2", 3, 0), ("vz", 2, 3), ("x1", 2, 0), ("vz", 2, 4), ("stage", 1), ("v2", 3),
    ("head", 1, 0), ("y2", 3, 1), ("head", 1, 1), ("vz", 2, 5), ("head", 1, 2), ("head", 1, 3), ("x1", 2, 1),
    ("v3", 3), ("vz", 3, 2), ("x1", 3, 0), ("vz", 3, 3), ("stage", 2), ("x1", 3, 1), ("head", 2, 0), ("head", 2, 1),
    ("vz", 3, 4), ("head", 2, 2), ("head", 2, 3), ("vz", 3, 5), ("stage", 3), ("head", 3, 0), ("head", 3, 1),
    ("head", 3, 2), ("head", 3, 3),
]


def rope_tables(place):
    positions = place * ROWS + jnp.arange(ROWS, dtype=jnp.int32)
    inverse = jnp.power(jnp.float32(500000.0), -jnp.arange(0, HW, 2, dtype=jnp.float32) / HW)
    angles = positions.astype(jnp.float32)[:, None] * inverse[None, :]
    cosine, sine = jnp.cos(angles), jnp.sin(angles)
    return jnp.concatenate([cosine, cosine], axis=1), jnp.concatenate([-sine, sine], axis=1)


def take(refs, *counts):
    refs = list(refs)
    out = []
    for count in counts:
        out.append(refs[:count] if count > 1 else refs[0])
        del refs[:count]
    return out


def guarded(condition, act):
    if condition is None:
        act()
    else:
        pl.when(condition)(act)


class Copy:
    def __init__(self, log, src, dst, send, recv, device, sends=None, takes=None):
        self.log, self.parts = log, (src, dst, send, recv, device)
        self.sends, self.takes = sends, takes
        self.landed = False

    def make(self):
        src, dst, send, recv, device = self.parts
        return pltpu.make_async_remote_copy(
            src_ref=src, dst_ref=dst, send_sem=send, recv_sem=recv, device_id=device, device_id_type=MESH
        )

    def start(self):
        guarded(self.sends, lambda: self.make().start())
        self.log.append(self)

    def land(self):
        guarded(self.takes, lambda: self.make().wait_recv())
        self.landed = True

    def sent(self):
        guarded(self.sends, lambda: self.make().wait_send())


def kernel(plan, vert_ref, slash_ref, tok_hbm, gain_ref, wq_hbm, wk_hbm, wv_hbm, cos_ref, sin_ref, out_hbm, *scratch):
    (
        tok, normed, w, kv, prev, ya, yb, xc, vy, vx, vz, qb, kall, vall, ob,
        local_sem, t_send, t_recv, f_send, p_send, p_recv, z_send, z_recv, y_send, y_recv,
        x_send, x_recv, vy_send, vy_recv, vx_send, vx_recv, vz_send, vz_recv, o_send, o_recv,
    ) = take(scratch, 4, 4, 1, 8, 8, 8, 8, 8, 4, 4, 4, 4, 1, 1, 4, *([1] * 20))
    s = lax.axis_index("seq")
    g = lax.axis_index("doc")
    core = lax.rem(g, 2)
    z = lax.rem(s, RING)
    row = s // RING
    y = lax.rem(row, COLS)
    x = row // COLS
    across = lax.rem(g - core + 2, 4)
    docs = [g, g + 1 - 2 * core, across, across + 1]

    def at(seq, doc):
        return {"seq": seq, "doc": doc}

    z_up = at(s - z + lax.rem(z + 1, RING), g)
    z_down = at(s - z + lax.rem(z + RING - 1, RING), g)
    y_up = at(s - y * RING + lax.rem(y + 1, COLS) * RING, g)
    y_far = at(s - y * RING + lax.rem(y + 2, COLS) * RING, g)
    y_down = at(s - y * RING + lax.rem(y + 3, COLS) * RING, g)
    x_far = at(lax.rem(s + LINE // 2, LINE), g)
    after = at(lax.rem(s + 1, LINE), g)
    before = at(lax.rem(s + LINE - 1, LINE), g)
    mates = [at(s, doc) for doc in docs]
    peer = at(s, across + core)

    log = []

    def remote(*parts, **ends):
        return Copy(log, *parts, **ends)

    loads = [
        pltpu.make_async_copy(tok_hbm, tok[0], local_sem.at[0]),
        pltpu.make_async_copy(wk_hbm, w.at[:, 0:HW], local_sem.at[1]),
        pltpu.make_async_copy(wv_hbm, w.at[:, HW : 2 * HW], local_sem.at[2]),
        pltpu.make_async_copy(wq_hbm, w.at[:, 2 * HW :], local_sem.at[3]),
    ]
    for load in loads:
        load.start()

    barrier = pltpu.get_barrier_semaphore()
    greeted = mates[1:] + [z_up, z_down, y_up, y_far, y_down, x_far, after, before]
    for device in greeted:
        pl.semaphore_signal(barrier, inc=1, device_id=device, device_id_type=MESH)
    pl.semaphore_wait(barrier, len(greeted))

    even, odd = core == 0, core == 1
    lower, upper = x == 0, x == 1
    gives_prev = jnp.logical_and(z == RING - 1, s < LINE - 1)
    takes_prev = jnp.logical_and(z == 0, s > 0)

    def rows_of(c):
        return pl.ds(c * PART, PART)

    def chunk_sem(k, c):
        return t_recv.at[(k - 2) * CHUNKS + c]

    crossing = [
        [
            remote(
                tok_hbm.at[rows_of(c)], tok[k].at[rows_of(c)], t_send.at[c], chunk_sem(k, c), peer,
                sends=even if k == 2 else odd,
            )
            for c in range(CHUNKS)
        ]
        for k in (2, 3)
    ]
    handed = [
        [
            remote(
                tok[k].at[rows_of(c)], tok[k].at[rows_of(c)], f_send.at[c], chunk_sem(k, c), mates[1],
                sends=even if k == 2 else odd,
            )
            for c in range(CHUNKS)
        ]
        for k in (2, 3)
    ]
    beside = remote(tok_hbm, tok[1], t_send.at[CHUNKS], t_recv.at[2 * CHUNKS], mates[1])

    def norm(k, start, count):
        def body(i, carry):
            at_rows = pl.ds(pl.multiple_of(start + i * 16, 16), 16)
            wide = tok[k][at_rows, :].astype(jnp.float32)
            scale = lax.rsqrt(jnp.sum(wide * wide, axis=-1, keepdims=True) * (1.0 / WIDTH) + 1e-05)
            normed[k][at_rows, :] = (wide * scale * gain_ref[...]).astype(jnp.bfloat16)
            return carry

        lax.fori_loop(0, count // 16, body, 0)

    def do_own(k):
        loads[0].wait()
        norm(0, 0, ROWS)

    def do_beside(k):
        beside.land()
        norm(1, 0, ROWS)

    def do_arrive(k, c):
        crossing[k - 2][c].land()
        handed[k - 2][c].start()
        handed[k - 2][c].landed = True
        if k == 2 and c == CHUNKS - 2:
            for copy in crossing[1]:
                copy.start()
        norm(k, c * PART, PART)

    def rotate(value, at_rows):
        return value * cos_ref[at_rows, :] + pltpu.roll(value, HW // 2, 1) * sin_ref[at_rows, :]

    ready = set()

    def loaded(*which):
        for i in which:
            if i not in ready:
                loads[i].wait()
                ready.add(i)

    def do_kv(k, h):
        loaded(1, 2)
        u = 2 * k + h
        at_rows = slice(h * HALF, (h + 1) * HALF)
        both = jnp.dot(normed[k][at_rows, :], w[:, 0 : 2 * HW], preferred_element_type=jnp.float32)
        kv[u][z, :, 0:HW] = rotate(both[:, 0:HW], at_rows).astype(jnp.bfloat16)
        kv[u][z, :, HW:] = both[:, HW:].astype(jnp.bfloat16)

    def do_q(k):
        loaded(3)
        wide = jnp.dot(normed[k][...], w[:, 2 * HW :], preferred_element_type=jnp.float32)
        for h in range(HEADS):
            qb[k][h * ROWS : (h + 1) * ROWS, :] = rotate(wide[:, h * HW : (h + 1) * HW], slice(0, ROWS)).astype(jnp.bfloat16)

    def ring(buf, k, send, recv):
        hops = {}
        for j in range(1, 5):
            for up in (True, False):
                if j == 4 and up != (k % 2 == 0):
                    continue
                place = lax.rem(z - (j - 1) + RING, RING) if up else lax.rem(z + (j - 1), RING)
                index = k * 7 + (0 if up else 3 + (k % 2 == 0)) + j - 1
                hops[up, j] = remote(
                    buf.at[place], buf.at[place], send.at[index], recv.at[index], z_up if up else z_down
                )
        return hops

    z_hops = [ring(kv[u], u, z_send, z_recv) for u in range(UNITS)]
    vz_hops = [ring(vz[k], k, vz_send, vz_recv) for k in range(DOCS)]

    def step(hops, j):
        for up in (True, False):
            if (up, j - 1) in hops:
                hops[up, j - 1].land()
            if (up, j) in hops:
                hops[up, j].start()

    def do_z(k, h, j):
        step(z_hops[2 * k + h], j)

    def do_vz(k, j):
        step(vz_hops[k], j)

    prevs = [
        remote(kv[u].at[z], prev[u], p_send.at[u], p_recv.at[u], after, sends=gives_prev, takes=takes_prev)
        for u in range(UNITS)
    ]

    def do_prev(k, h):
        prevs[2 * k + h].start()

    offset = [[slash_ref[docs[k], g, t] for t in range(SLOTS)] for k in range(DOCS)]
    vertical = [[vert_ref[docs[k], g, i] for i in range(4)] for k in range(DOCS)]
    mine = [vert_ref[docs[k], g, lax.rem(z, 4)] for k in range(DOCS)]
    shift = [[(offset[k][t] - z + RING - 1) // RING for t in range(SLOTS)] for k in range(DOCS)]

    def turns(k, t):
        steps = lax.rem(shift[k][t], COLS)
        return steps if t < 2 else lax.rem(COLS - steps, COLS)

    y_near = [
        [
            remote(ya[u].at[0, 0:2], ya[u].at[1, 0:2], y_send.at[u * 3], y_recv.at[u * 3], y_up),
            remote(ya[u].at[0, 2:4], ya[u].at[1, 2:4], y_send.at[u * 3 + 1], y_recv.at[u * 3 + 1], y_down),
        ]
        for u in range(UNITS)
    ]
    y_over = [
        remote(yb[u].at[0], yb[u].at[1], y_send.at[u * 3 + 2], y_recv.at[u * 3 + 2], y_far) for u in range(UNITS)
    ]
    x_over = [
        remote(xc[u].at[0], xc[u].at[1], x_send.at[u], x_recv.at[u], x_far, sends=lower, takes=upper)
        for u in range(UNITS)
    ]
    vy_over = [
        [
            remote(vy[k].at[y], vy[k].at[y], vy_send.at[k * 3 + i], vy_recv.at[k * 3 + i], device)
            for i, device in enumerate((y_up, y_far, y_down))
        ]
        for k in range(DOCS)
    ]
    vx_over = [
        remote(vx[k].at[0], vx[k].at[1], vx_send.at[k], vx_recv.at[k], x_far, sends=lower, takes=upper)
        for k in range(DOCS)
    ]

    def do_y1(k, h):
        u = 2 * k + h
        for t in range(SLOTS):
            ya[u][0, t] = kv[u][lax.rem(z - offset[k][t] + LINE, RING)]
        for copy in y_near[u]:
            copy.start()

    def do_y2(k, h):
        u = 2 * k + h
        for copy in y_near[u]:
            copy.land()
        for t in range(SLOTS):
            yb[u][0, t] = ya[u][lax.rem(turns(k, t), 2), t]
        y_over[u].start()

    def do_x1(k, h):
        u = 2 * k + h
        y_over[u].land()
        for t in range(SLOTS):
            xc[u][0, t] = yb[u][turns(k, t) // 2, t]
        x_over[u].start()

    def do_v1(k):
        for h in range(2):

            @pl.when(z // 4 == h)
            def _():
                vy[k][y] = kv[2 * k + h][lax.rem(mine[k], RING)]

        for copy in vy_over[k]:
            copy.start()

    def do_v2(k):
        for copy in vy_over[k]:
            copy.land()
        vx[k][0] = vy[k][lax.rem(mine[k] // RING, COLS)]
        vx_over[k].start()

    def do_v3(k):
        vx_over[k].land()
        vz[k][z] = vx[k][x * (mine[k] < LINE // 2).astype(jnp.int32)]
        do_vz(k, 1)

    def columns(i):
        return pl.ds(pl.multiple_of(g * 512 + i * HW, HW), HW)

    out_own = [
        pltpu.make_async_copy(ob[0].at[i], out_hbm.at[:, columns(i)], local_sem.at[4 + i]) for i in range(HEADS)
    ]

    def out_copy(k, i, receive):
        return remote(
            ob[k].at[i], out_hbm.at[:, columns(i)], o_send.at[(k - 1) * HEADS + i], o_recv.at[receive * HEADS + i],
            mates[k],
        )

    out_sent = [None] + [[out_copy(k, i, 0 if k == 1 else 1 + core) for i in range(HEADS)] for k in range(1, DOCS)]
    out_got = [out_copy(1, i, source) for source in range(3) for i in range(HEADS)]

    low = jnp.float32(-jnp.inf)

    bias = {}

    def do_stage(k):
        for h in range(2):
            u = 2 * k + h
            prevs[u].land()
            x_over[u].land()

            def put(i, value):
                at_rows = slice(i * ROWS + h * HALF, i * ROWS + (h + 1) * HALF)
                kall[at_rows, :] = value[:, 0:HW]
                vall[at_rows, :] = value[:, HW:]

            put(0, kv[u][z])

            @pl.when(z > 0)
            def _():
                put(1, kv[u][lax.rem(z + RING - 1, RING)])

            @pl.when(takes_prev)
            def _():
                put(1, prev[u][...])

            @pl.when(s == 0)
            def _():
                put(1, jnp.zeros((HALF, 2 * HW), jnp.bfloat16))

            for t in range(SLOTS):
                put(2 + t, xc[u][x * (shift[k][t] > y).astype(jnp.int32), t])
            for i in range(4):
                put(2 + SLOTS + i, vz[k][i + 4 * h])
        allowed = [s >= 1] + [s >= offset[k][t] for t in range(SLOTS)]
        for i in range(4):
            good = vertical[k][i] < s - 1
            for t in range(SLOTS):
                good = jnp.logical_and(good, vertical[k][i] != s - offset[k][t])
            allowed.append(good)
        bias[k] = [jnp.where(good, jnp.float32(0.0), low) for good in allowed]

    def do_head(k, i):
        blocks = 2 + SLOTS + 4
        causal = lax.broadcasted_iota(jnp.int32, (ROWS, ROWS), 1) <= lax.broadcasted_iota(jnp.int32, (ROWS, ROWS), 0)
        scores = lax.dot_general(
            qb[k][i * ROWS : (i + 1) * ROWS, :],
            kall[...],
            (((1,), (1,)), ((), ())),
            preferred_element_type=jnp.float32,
        ) * (HW ** (-0.5))
        tiles = [scores[:, n * ROWS : (n + 1) * ROWS] for n in range(blocks)]
        tiles = [jnp.where(causal, tiles[0], low)] + [tiles[n] + bias[k][n - 1] for n in range(1, blocks)]
        highest = tiles[0]
        for tile in tiles[1:]:
            highest = jnp.maximum(highest, tile)
        highest = jnp.max(highest, axis=1, keepdims=True)
        raised = [jnp.exp(tile - highest) for tile in tiles]
        total = raised[0]
        for tile in raised[1:]:
            total = total + tile
        total = jnp.sum(total, axis=1, keepdims=True)
        weights = jnp.concatenate([tile.astype(jnp.bfloat16) for tile in raised], axis=1)
        mixed = jnp.dot(weights, vall[...], preferred_element_type=jnp.float32) / total
        ob[k][i] = mixed.astype(jnp.bfloat16)
        if k == 0:
            out_own[i].start()
        else:
            out_sent[k][i].start()
            out_sent[k][i].landed = True

    for copy in crossing[0]:
        copy.start()
    beside.start()
    does = {
        "own": do_own, "beside": do_beside, "arrive": do_arrive, "kv": do_kv, "q": do_q, "z": do_z, "vz": do_vz,
        "prev": do_prev, "y1": do_y1, "y2": do_y2, "x1": do_x1, "v1": do_v1, "v2": do_v2, "v3": do_v3,
        "stage": do_stage, "head": do_head,
    }
    for name, *which in plan:
        does[name](*which)

    loaded(1, 2, 3)
    for copy in log:
        if not copy.landed:
            copy.land()
        copy.sent()
    for copy in out_own:
        copy.wait()
    for copy in out_got:
        copy.land()


def layer(plan, collective_id, tokens, norm_gain, w_query, key_weight, value_weight, vertical_blocks, slash_offsets):
    cosine, sine = rope_tables(lax.axis_index("seq"))
    bf16 = jnp.bfloat16
    unit = (HALF, 2 * HW)
    dma = pltpu.SemaphoreType.DMA

    def many(shape):
        return [pltpu.VMEM(shape, bf16)] * DOCS

    scratch = (
        many((ROWS, WIDTH))
        + many((ROWS, WIDTH))
        + [pltpu.VMEM((WIDTH, 6 * HW), bf16)]
        + many((RING,) + unit) * 2
        + many(unit) * 2
        + many((2, SLOTS) + unit) * 6
        + many((COLS,) + unit)
        + many((2,) + unit)
        + many((RING,) + unit)
        + many((HEADS * ROWS, HW))
        + [pltpu.VMEM((10 * ROWS, HW), bf16)] * 2
        + many((HEADS, ROWS, HW))
        + [dma((4 + HEADS,)), dma((CHUNKS + 1,)), dma((2 * CHUNKS + 1,)), dma((CHUNKS,))]
    )
    for count in (8, 56, 24, 8, 12, 4, 28, 12):
        scratch += [dma((count,))] * 2
    smem = pl.BlockSpec(memory_space=pltpu.SMEM)
    vmem = pl.BlockSpec(memory_space=pltpu.VMEM)
    hbm = pl.BlockSpec(memory_space=pl.ANY)
    out = pl.pallas_call(
        functools.partial(kernel, plan),
        out_shape=jax.ShapeDtypeStruct((ROWS, DOCS * HEADS * HW), bf16),
        in_specs=[smem, smem, hbm, vmem, hbm, hbm, hbm, vmem, vmem],
        out_specs=hbm,
        scratch_shapes=scratch,
        compiler_params=pltpu.CompilerParams(
            collective_id=collective_id, has_side_effects=True, vmem_limit_bytes=60 * 1024 * 1024
        ),
    )(
        vertical_blocks, slash_offsets, tokens[0], norm_gain[None, :], w_query, key_weight, value_weight, cosine, sine
    )
    return out[None]


IN_SPECS = (
    P("doc", "seq", None),
    P(),
    P(None, "doc"),
    P(None, "doc"),
    P(None, "doc"),
    P(),
    P(),
)


def solution(mesh):
    return jax.shard_map(
        functools.partial(layer, PLAN, 0),
        mesh=mesh,
        in_specs=IN_SPECS,
        out_specs=P("doc", "seq", None),
        check_vma=False,
    )
```

time: 111 us -> 99.2 us (0.89)
  Pallas kernels: 107 us -> 94.7 us
    pallas_call x1, Pallas kernels: 107 us -> 94.7 us  [layer(): pl.pallas_call(functools.partial(kernel, plan), out_shape=jax.ShapeDtypeS...]
where the time goes in v4:
time: 99.2 us; the launch traced here: 97.7 us
  Pallas kernels  94.7 us (95%)
  local copies, waits for them, and re-layouts  1.88 us (2%)
  other arithmetic  1.08 us (1%)
    pallas_call x1, Pallas kernels, layer(): pl.pallas_call(functools.partial(kernel, plan), out_shape=jax.ShapeDtypeS...  94.7 us

profile of v4, /device:TPU:5, one launch (start us, length us, event | category | flops | bytes accessed | tf_op | source)
XLA Modules:
  0.0 97.7 jit_solution(3830602121465091468)
XLA Ops:
  0.0 0.3 fusion
  0.3 0.7 pad_maximum_fusion
  1.1 94.7 %shard_map.73 = bf16[128,2048]{1,0:T(8,128)(2,1)} custom-call(s32[4,4,4]{2,1,0:T(4,128)} %vert_ref.1, s32[4,4,4]{2,1,0:T(4,128)} %slash_ref.1, bf16[128,4096]{1,0:T(8,128)(2,1)} %bitcast.4, f32[1,4096]{1,0:T(1,128)} %bitcast.5, bf16[4096,512]{1,0:T(8,128)(2,1)} %wq_hbm.1, bf16[4096,128]{1,0:T(8,128)(2,1)} %wk_hbm.1, bf16[4096,128]{1,0:T(8,128)(2,1)} %wv_hbm.1, ...), custom_call_target="tpu_custom_call" | custom-call | tf_op jit(solution)/shard_map/pallas_call | solution.py:484
  95.8 1.9 %copy.9 = bf16[1,128,2048]{2,1,0:T(8,128)(2,1)} copy(bf16[1,128,2048]{2,1,0:T(8,128)(2,1)} %bitcast.3) | data formatting | bytes 1048576
  (2 shorter events, 0.0 us)

commit v5 on v4

--- a/solution.py
+++ b/solution.py
@@ -23,26 +23,21 @@
 LINE = 64
 
 PLAN = [
-    ("own", 0), ("kv", 0, 0), ("kv", 0, 1), ("z", 0, 0, 1), ("prev", 0, 0), ("z", 0, 1, 1), ("prev", 0, 1), ("q", 0),
-    ("beside", 1), ("kv", 1, 0), ("arrive", 2, 0), ("kv", 1, 1), ("z", 1, 0, 1), ("prev", 1, 0), ("z", 1, 1, 1),
-    ("prev", 1, 1), ("z", 0, 0, 2), ("z", 0, 1, 2), ("q", 1), ("arrive", 2, 1), ("kv", 2, 0), ("z", 2, 0, 1),
-    ("prev", 2, 0), ("z", 1, 0, 2), ("z", 1, 1, 2), ("z", 0, 0, 3), ("z", 0, 1, 3), ("arrive", 2, 2), ("z", 2, 0, 2),
-    ("z", 1, 0, 3), ("z", 1, 1, 3), ("z", 0, 0, 4), ("arrive", 2, 3), ("kv", 2, 1), ("z", 2, 1, 1), ("prev", 2, 1),
-    ("z", 0, 1, 4), ("q", 2), ("z", 2, 0, 3), ("z", 1, 0, 4), ("z", 1, 1, 4), ("z", 0, 0, 5), ("y1", 0, 0),
-    ("arrive", 3, 0), ("z", 0, 1, 5), ("z", 2, 1, 2), ("v1", 0), ("y1", 0, 1), ("z", 2, 0, 4), ("z", 1, 0, 5),
-    ("z", 1, 1, 5), ("v1", 1), ("y1", 1, 0), ("y1", 1, 1), ("arrive", 3, 1), ("kv", 3, 0), ("z", 3, 0, 1),
-    ("prev", 3, 0), ("z", 2, 1, 3), ("y2", 0, 0), ("z", 2, 0, 5), ("y1", 2, 0), ("arrive", 3, 2), ("y2", 0, 1),
-    ("z", 3, 0, 2), ("z", 2, 1, 4), ("arrive", 3, 3), ("kv", 3, 1), ("z", 3, 0, 3), ("z", 3, 1, 1), ("prev", 3, 1),
-    ("z", 2, 1, 5), ("v1", 2), ("y1", 2, 1), ("v2", 1), ("y2", 1, 0), ("v2", 0), ("q", 3), ("y2", 1, 1),
-    ("z", 3, 0, 4), ("z", 3, 1, 2), ("v3", 1), ("v3", 0), ("x1", 0, 0), ("z", 3, 0, 5), ("y1", 3, 0), ("y2", 2, 0),
-    ("z", 3, 1, 3), ("vz", 1, 2), ("vz", 0, 2), ("z", 3, 1, 4), ("vz", 1, 3), ("x1", 0, 1), ("vz", 0, 3), ("v2", 2),
-    ("z", 3, 1, 5), ("v1", 3), ("y1", 3, 1), ("y2", 2, 1), ("vz", 1, 4), ("vz", 0, 4), ("vz", 1, 5), ("vz", 0, 5),
-    ("stage", 0), ("x1", 1, 0), ("v3", 2), ("head", 0, 0), ("head", 0, 1), ("head", 0, 2), ("vz", 2, 2),
-    ("x1", 1, 1), ("head", 0, 3), ("y2", 3, 0), ("vz", 2, 3), ("x1", 2, 0), ("vz", 2, 4), ("stage", 1), ("v2", 3),
-    ("head", 1, 0), ("y2", 3, 1), ("head", 1, 1), ("vz", 2, 5), ("head", 1, 2), ("head", 1, 3), ("x1", 2, 1),
-    ("v3", 3), ("vz", 3, 2), ("x1", 3, 0), ("vz", 3, 3), ("stage", 2), ("x1", 3, 1), ("head", 2, 0), ("head", 2, 1),
-    ("vz", 3, 4), ("head", 2, 2), ("head", 2, 3), ("vz", 3, 5), ("stage", 3), ("head", 3, 0), ("head", 3, 1),
-    ("head", 3, 2), ("head", 3, 3),
+    ("own", 0), ("kv", 0, 0), ("z", 0, 0, 1), ("kv", 0, 1), ("z", 0, 1, 1), ("prev", 0, 0), ("prev", 0, 1), ("q", 0),
+    ("beside", 1), ("kv", 1, 0), ("z", 1, 0, 1), ("kv", 1, 1), ("z", 1, 1, 1), ("z", 0, 0, 2), ("prev", 1, 0),
+    ("prev", 1, 1), ("arrive", 2, 0), ("q", 1), ("z", 0, 1, 2), ("arrive", 2, 1), ("kv", 2, 0), ("z", 2, 0, 1),
+    ("prev", 2, 0), ("z", 1, 0, 2), ("arrive", 2, 2), ("z", 1, 1, 2), ("z", 0, 0, 3), ("y1", 0, 0), ("z", 0, 1, 3),
+    ("v1", 0), ("y1", 0, 1), ("arrive", 2, 3), ("kv", 2, 1), ("z", 2, 1, 1), ("prev", 2, 1), ("q", 2),
+    ("z", 2, 0, 2), ("arrive", 3, 0), ("y2", 0, 0), ("z", 1, 0, 3), ("y1", 1, 0), ("z", 1, 1, 3), ("v1", 1),
+    ("y1", 1, 1), ("v2", 0), ("y2", 0, 1), ("arrive", 3, 1), ("kv", 3, 0), ("z", 3, 0, 1), ("z", 2, 1, 2),
+    ("prev", 3, 0), ("z", 2, 0, 3), ("y1", 2, 0), ("arrive", 3, 2), ("y2", 1, 0), ("z", 3, 0, 2), ("arrive", 3, 3),
+    ("kv", 3, 1), ("z", 3, 1, 1), ("v2", 1), ("prev", 3, 1), ("x1", 0, 0), ("y2", 1, 1), ("q", 3), ("z", 2, 1, 3),
+    ("v1", 2), ("y1", 2, 1), ("v3", 0), ("z", 3, 0, 3), ("y1", 3, 0), ("x1", 0, 1), ("v3", 1), ("y2", 2, 0),
+    ("z", 3, 1, 2), ("vz", 0, 2), ("x1", 1, 0), ("vz", 1, 2), ("x1", 1, 1), ("z", 3, 1, 3), ("v1", 3), ("y1", 3, 1),
+    ("v2", 2), ("vz", 0, 3), ("y2", 2, 1), ("stage", 0), ("head", 0, 0), ("y2", 3, 0), ("vz", 1, 3), ("head", 0, 1),
+    ("stage", 1), ("v3", 2), ("x1", 2, 0), ("head", 1, 0), ("v2", 3), ("y2", 3, 1), ("head", 1, 1), ("vz", 2, 2),
+    ("x1", 2, 1), ("v3", 3), ("x1", 3, 0), ("vz", 2, 3), ("x1", 3, 1), ("vz", 3, 2), ("stage", 2), ("head", 2, 0),
+    ("head", 2, 1), ("vz", 3, 3), ("stage", 3), ("head", 3, 0), ("head", 3, 1),
 ]
 
 
@@ -115,6 +110,8 @@
 
     z_up = at(s - z + lax.rem(z + 1, RING), g)
     z_down = at(s - z + lax.rem(z + RING - 1, RING), g)
+    z_up_two = at(s - z + lax.rem(z + 2, RING), g)
+    z_down_two = at(s - z + lax.rem(z + RING - 2, RING), g)
     y_up = at(s - y * RING + lax.rem(y + 1, COLS) * RING, g)
     y_far = at(s - y * RING + lax.rem(y + 2, COLS) * RING, g)
     y_down = at(s - y * RING + lax.rem(y + 3, COLS) * RING, g)
@@ -139,7 +136,7 @@
         load.start()
 
     barrier = pltpu.get_barrier_semaphore()
-    greeted = mates[1:] + [z_up, z_down, y_up, y_far, y_down, x_far, after, before]
+    greeted = mates[1:] + [z_up, z_down, z_up_two, z_down_two, y_up, y_far, y_down, x_far, after, before]
     for device in greeted:
         pl.semaphore_signal(barrier, inc=1, device_id=device, device_id_type=MESH)
     pl.semaphore_wait(barrier, len(greeted))
@@ -230,27 +227,24 @@
             qb[k][h * ROWS : (h + 1) * ROWS, :] = rotate(wide[:, h * HW : (h + 1) * HW], slice(0, ROWS)).astype(jnp.bfloat16)
 
     def ring(buf, k, send, recv):
-        hops = {}
-        for j in range(1, 5):
-            for up in (True, False):
-                if j == 4 and up != (k % 2 == 0):
-                    continue
-                place = lax.rem(z - (j - 1) + RING, RING) if up else lax.rem(z + (j - 1), RING)
-                index = k * 7 + (0 if up else 3 + (k % 2 == 0)) + j - 1
-                hops[up, j] = remote(
-                    buf.at[place], buf.at[place], send.at[index], recv.at[index], z_up if up else z_down
-                )
-        return hops
+        behind, ahead = lax.rem(z + RING - 2, RING), lax.rem(z + 2, RING)
+        routes = [(z, z_up_two), (z, z_down_two), (z, z_up), (z, z_down)]
+        routes += [(behind, z_up_two) if k % 2 == 0 else (ahead, z_down_two), (behind, z_up), (ahead, z_down)]
+        return [
+            remote(buf.at[place], buf.at[place], send.at[k * 7 + i], recv.at[k * 7 + i], device)
+            for i, (place, device) in enumerate(routes)
+        ]
 
     z_hops = [ring(kv[u], u, z_send, z_recv) for u in range(UNITS)]
     vz_hops = [ring(vz[k], k, vz_send, vz_recv) for k in range(DOCS)]
 
     def step(hops, j):
-        for up in (True, False):
-            if (up, j - 1) in hops:
-                hops[up, j - 1].land()
-            if (up, j) in hops:
-                hops[up, j].start()
+        lands = ((), (0, 1), (2, 3, 4, 5, 6))[j - 1]
+        starts = (range(4), range(4, 7), ())[j - 1]
+        for i in lands:
+            hops[i].land()
+        for i in starts:
+            hops[i].start()
 
     def do_z(k, h, j):
         step(z_hops[2 * k + h], j)
@@ -401,34 +395,35 @@
             allowed.append(good)
         bias[k] = [jnp.where(good, jnp.float32(0.0), low) for good in allowed]
 
-    def do_head(k, i):
+    def do_head(k, pair):
         blocks = 2 + SLOTS + 4
         causal = lax.broadcasted_iota(jnp.int32, (ROWS, ROWS), 1) <= lax.broadcasted_iota(jnp.int32, (ROWS, ROWS), 0)
-        scores = lax.dot_general(
-            qb[k][i * ROWS : (i + 1) * ROWS, :],
-            kall[...],
-            (((1,), (1,)), ((), ())),
-            preferred_element_type=jnp.float32,
-        ) * (HW ** (-0.5))
-        tiles = [scores[:, n * ROWS : (n + 1) * ROWS] for n in range(blocks)]
-        tiles = [jnp.where(causal, tiles[0], low)] + [tiles[n] + bias[k][n - 1] for n in range(1, blocks)]
-        highest = tiles[0]
-        for tile in tiles[1:]:
-            highest = jnp.maximum(highest, tile)
-        highest = jnp.max(highest, axis=1, keepdims=True)
-        raised = [jnp.exp(tile - highest) for tile in tiles]
-        total = raised[0]
-        for tile in raised[1:]:
-            total = total + tile
-        total = jnp.sum(total, axis=1, keepdims=True)
-        weights = jnp.concatenate([tile.astype(jnp.bfloat16) for tile in raised], axis=1)
-        mixed = jnp.dot(weights, vall[...], preferred_element_type=jnp.float32) / total
-        ob[k][i] = mixed.astype(jnp.bfloat16)
-        if k == 0:
-            out_own[i].start()
-        else:
-            out_sent[k][i].start()
-            out_sent[k][i].landed = True
+        for i in (2 * pair, 2 * pair + 1):
+            scores = lax.dot_general(
+                qb[k][i * ROWS : (i + 1) * ROWS, :],
+                kall[...],
+                (((1,), (1,)), ((), ())),
+                preferred_element_type=jnp.float32,
+            )
+            tiles = [scores[:, n * ROWS : (n + 1) * ROWS] for n in range(blocks)]
+            tiles = [jnp.where(causal, tiles[0], low)] + [tiles[n] + bias[k][n - 1] for n in range(1, blocks)]
+            highest = tiles[0]
+            for tile in tiles[1:]:
+                highest = jnp.maximum(highest, tile)
+            highest = jnp.max(highest, axis=1, keepdims=True)
+            raised = [jnp.exp2((tile - highest) * (HW ** (-0.5) * 1.4426950408889634)) for tile in tiles]
+            total = raised[0]
+            for tile in raised[1:]:
+                total = total + tile
+            total = jnp.sum(total, axis=1, keepdims=True)
+            weights = jnp.concatenate([tile.astype(jnp.bfloat16) for tile in raised], axis=1)
+            mixed = jnp.dot(weights, vall[...], preferred_element_type=jnp.float32) / total
+            ob[k][i] = mixed.astype(jnp.bfloat16)
+            if k == 0:
+                out_own[i].start()
+            else:
+                out_sent[k][i].start()
+                out_sent[k][i].landed = True
 
     for copy in crossing[0]:
         copy.start()

time: 99.2 us -> 91.7 us (0.924); the launches traced: 97.7 us -> 91.5 us
  Pallas kernels: 94.7 us -> 88.6 us
    pallas_call x1, Pallas kernels: 94.7 us -> 88.6 us  [layer(): pl.pallas_call(functools.partial(kernel, plan), out_shape=jax.ShapeDtypeS...]
where the time goes in v5:
time: 91.7 us; the launch traced here: 91.5 us
  Pallas kernels  88.6 us (97%)
  local copies, waits for them, and re-layouts  1.88 us (2%)
  other arithmetic  1.08 us (1%)
    pallas_call x1, Pallas kernels, layer(): pl.pallas_call(functools.partial(kernel, plan), out_shape=jax.ShapeDtypeS...  88.6 us
    unnamed x1, local copies, waits for them, and re-layouts  1.88 us

profile of v5, /device:TPU:5, one launch (start us, length us, event | category | flops | bytes accessed | tf_op | source)
XLA Modules:
  0.0 91.5 jit_solution(3715837957016729170)
XLA Ops:
  0.0 0.3 fusion
  0.3 0.7 pad_maximum_fusion
  1.1 88.6 %shard_map.73 = bf16[128,2048]{1,0:T(8,128)(2,1)} custom-call(s32[4,4,4]{2,1,0:T(4,128)} %vert_ref.1, s32[4,4,4]{2,1,0:T(4,128)} %slash_ref.1, bf16[128,4096]{1,0:T(8,128)(2,1)} %bitcast.4, f32[1,4096]{1,0:T(1,128)} %bitcast.5, bf16[4096,512]{1,0:T(8,128)(2,1)} %wq_hbm.1, bf16[4096,128]{1,0:T(8,128)(2,1)} %wk_hbm.1, bf16[4096,128]{1,0:T(8,128)(2,1)} %wv_hbm.1, ...), custom_call_target="tpu_custom_call" | custom-call | tf_op jit(solution)/shard_map/pallas_call | solution.py:479
  89.7 1.9 %copy.9 = bf16[1,128,2048]{2,1,0:T(8,128)(2,1)} copy(bf16[1,128,2048]{2,1,0:T(8,128)(2,1)} %bitcast.3) | data formatting | bytes 1048576
  (2 shorter events, 0.0 us)

commit v6 on v5

--- a/solution.py
+++ b/solution.py
@@ -2,6 +2,7 @@
 
 import jax
 import jax.numpy as jnp
+import numpy as np
 from jax import lax
 from jax.experimental import pallas as pl
 from jax.experimental.pallas import tpu as pltpu
@@ -23,30 +24,30 @@
 LINE = 64
 
 PLAN = [
-    ("own", 0), ("kv", 0, 0), ("z", 0, 0, 1), ("kv", 0, 1), ("z", 0, 1, 1), ("prev", 0, 0), ("prev", 0, 1), ("q", 0),
-    ("beside", 1), ("kv", 1, 0), ("z", 1, 0, 1), ("kv", 1, 1), ("z", 1, 1, 1), ("z", 0, 0, 2), ("prev", 1, 0),
-    ("prev", 1, 1), ("arrive", 2, 0), ("q", 1), ("z", 0, 1, 2), ("arrive", 2, 1), ("kv", 2, 0), ("z", 2, 0, 1),
-    ("prev", 2, 0), ("z", 1, 0, 2), ("arrive", 2, 2), ("z", 1, 1, 2), ("z", 0, 0, 3), ("y1", 0, 0), ("z", 0, 1, 3),
-    ("v1", 0), ("y1", 0, 1), ("arrive", 2, 3), ("kv", 2, 1), ("z", 2, 1, 1), ("prev", 2, 1), ("q", 2),
-    ("z", 2, 0, 2), ("arrive", 3, 0), ("y2", 0, 0), ("z", 1, 0, 3), ("y1", 1, 0), ("z", 1, 1, 3), ("v1", 1),
-    ("y1", 1, 1), ("v2", 0), ("y2", 0, 1), ("arrive", 3, 1), ("kv", 3, 0), ("z", 3, 0, 1), ("z", 2, 1, 2),
-    ("prev", 3, 0), ("z", 2, 0, 3), ("y1", 2, 0), ("arrive", 3, 2), ("y2", 1, 0), ("z", 3, 0, 2), ("arrive", 3, 3),
-    ("kv", 3, 1), ("z", 3, 1, 1), ("v2", 1), ("prev", 3, 1), ("x1", 0, 0), ("y2", 1, 1), ("q", 3), ("z", 2, 1, 3),
-    ("v1", 2), ("y1", 2, 1), ("v3", 0), ("z", 3, 0, 3), ("y1", 3, 0), ("x1", 0, 1), ("v3", 1), ("y2", 2, 0),
-    ("z", 3, 1, 2), ("vz", 0, 2), ("x1", 1, 0), ("vz", 1, 2), ("x1", 1, 1), ("z", 3, 1, 3), ("v1", 3), ("y1", 3, 1),
-    ("v2", 2), ("vz", 0, 3), ("y2", 2, 1), ("stage", 0), ("head", 0, 0), ("y2", 3, 0), ("vz", 1, 3), ("head", 0, 1),
-    ("stage", 1), ("v3", 2), ("x1", 2, 0), ("head", 1, 0), ("v2", 3), ("y2", 3, 1), ("head", 1, 1), ("vz", 2, 2),
-    ("x1", 2, 1), ("v3", 3), ("x1", 3, 0), ("vz", 2, 3), ("x1", 3, 1), ("vz", 3, 2), ("stage", 2), ("head", 2, 0),
-    ("head", 2, 1), ("vz", 3, 3), ("stage", 3), ("head", 3, 0), ("head", 3, 1),
+    ("own", 0), ("kv", 0, 0), ("kv", 0, 1), ("z", 0, 0, 1), ("z", 0, 1, 1), ("prev", 0, 0), ("prev", 0, 1), ("q", 0),
+    ("beside", 1), ("kv", 1, 0), ("kv", 1, 1), ("prev", 1, 0), ("prev", 1, 1), ("arrive", 2, 0), ("z", 0, 0, 2),
+    ("z", 1, 0, 1), ("q", 1), ("z", 0, 1, 2), ("z", 1, 1, 1), ("arrive", 2, 1), ("kv", 2, 0), ("z", 2, 0, 1),
+    ("prev", 2, 0), ("z", 0, 0, 3), ("y1", 0, 0), ("arrive", 2, 2), ("z", 1, 0, 2), ("z", 0, 1, 3), ("v1", 0),
+    ("y1", 0, 1), ("arrive", 2, 3), ("kv", 2, 1), ("y2", 0, 0), ("z", 1, 1, 2), ("z", 2, 1, 1), ("prev", 2, 1),
+    ("q", 2), ("z", 2, 0, 2), ("arrive", 3, 0), ("v2", 0), ("y2", 0, 1), ("z", 1, 0, 3), ("y1", 1, 0),
+    ("z", 1, 1, 3), ("v1", 1), ("y1", 1, 1), ("arrive", 3, 1), ("kv", 3, 0), ("z", 3, 0, 1), ("prev", 3, 0),
+    ("z", 2, 1, 2), ("arrive", 3, 2), ("z", 2, 0, 3), ("y1", 2, 0), ("y2", 1, 0), ("z", 3, 0, 2), ("arrive", 3, 3),
+    ("kv", 3, 1), ("x1", 0, 0), ("x1", 0, 1), ("z", 3, 1, 1), ("v2", 1), ("prev", 3, 1), ("q", 3), ("y2", 1, 1),
+    ("z", 2, 1, 3), ("v1", 2), ("y1", 2, 1), ("v3", 0), ("y2", 2, 0), ("z", 3, 0, 3), ("y1", 3, 0), ("z", 3, 1, 2),
+    ("x1", 1, 0), ("vz", 0, 2), ("x1", 1, 1), ("v3", 1), ("v2", 2), ("z", 3, 1, 3), ("v1", 3), ("y1", 3, 1),
+    ("y2", 2, 1), ("vz", 0, 3), ("stage", 0), ("head", 0, 0), ("x1", 2, 0), ("vz", 1, 2), ("y2", 3, 0),
+    ("head", 0, 1), ("v3", 2), ("v2", 3), ("y2", 3, 1), ("vz", 1, 3), ("stage", 1), ("head", 1, 0), ("x1", 2, 1),
+    ("v3", 3), ("vz", 2, 2), ("head", 1, 1), ("x1", 3, 0), ("vz", 3, 2), ("x1", 3, 1), ("vz", 2, 3), ("stage", 2),
+    ("head", 2, 0), ("head", 2, 1), ("vz", 3, 3), ("stage", 3), ("head", 3, 0), ("head", 3, 1),
 ]
 
 
-def rope_tables(place):
-    positions = place * ROWS + jnp.arange(ROWS, dtype=jnp.int32)
-    inverse = jnp.power(jnp.float32(500000.0), -jnp.arange(0, HW, 2, dtype=jnp.float32) / HW)
-    angles = positions.astype(jnp.float32)[:, None] * inverse[None, :]
-    cosine, sine = jnp.cos(angles), jnp.sin(angles)
-    return jnp.concatenate([cosine, cosine], axis=1), jnp.concatenate([-sine, sine], axis=1)
+def rope_constants():
+    inverse = 500000.0 ** (-np.arange(0, HW, 2, dtype=np.float64) / HW)
+    inverse = np.concatenate([inverse, inverse]).astype(np.float32).astype(np.float64)[None, :]
+    near = np.arange(ROWS, dtype=np.float64)[:, None] * inverse
+    far = np.arange(LINE, dtype=np.float64)[:, None] * ROWS * inverse
+    return [jnp.asarray(f(angle), jnp.float32) for angle in (near, far) for f in (np.cos, np.sin)]
 
 
 def take(refs, *counts):
@@ -89,12 +90,12 @@
         guarded(self.sends, lambda: self.make().wait_send())
 
 
-def kernel(plan, vert_ref, slash_ref, tok_hbm, gain_ref, wq_hbm, wk_hbm, wv_hbm, cos_ref, sin_ref, out_hbm, *scratch):
+def kernel(plan, vert_ref, slash_ref, tok_hbm, gain_ref, wq_hbm, wk_hbm, wv_hbm, near_cos, near_sin, far_cos, far_sin, out_ref, *scratch):
     (
-        tok, normed, w, kv, prev, ya, yb, xc, vy, vx, vz, qb, kall, vall, ob,
+        tok, normed, w, kv, prev, ya, yb, xc, vy, vx, vz, qb, kall, vall, ob, cos_ref, sin_ref,
         local_sem, t_send, t_recv, f_send, p_send, p_recv, z_send, z_recv, y_send, y_recv,
         x_send, x_recv, vy_send, vy_recv, vx_send, vx_recv, vz_send, vz_recv, o_send, o_recv,
-    ) = take(scratch, 4, 4, 1, 8, 8, 8, 8, 8, 4, 4, 4, 4, 1, 1, 4, *([1] * 20))
+    ) = take(scratch, 4, 4, 1, 8, 8, 8, 8, 8, 4, 4, 4, 4, 1, 1, 4, 1, 1, *([1] * 20))
     s = lax.axis_index("seq")
     g = lax.axis_index("doc")
     core = lax.rem(g, 2)
@@ -185,6 +186,10 @@
         lax.fori_loop(0, count // 16, body, 0)
 
     def do_own(k):
+        turn_cos, turn_sin = far_cos[pl.ds(s, 1), :], far_sin[pl.ds(s, 1), :]
+        sign = jnp.where(lax.broadcasted_iota(jnp.int32, (1, HW), 1) < HW // 2, -1.0, 1.0)
+        cos_ref[...] = near_cos[...] * turn_cos - near_sin[...] * turn_sin
+        sin_ref[...] = (near_sin[...] * turn_cos + near_cos[...] * turn_sin) * sign
         loads[0].wait()
         norm(0, 0, ROWS)
 
@@ -342,12 +347,12 @@
         return pl.ds(pl.multiple_of(g * 512 + i * HW, HW), HW)
 
     out_own = [
-        pltpu.make_async_copy(ob[0].at[i], out_hbm.at[:, columns(i)], local_sem.at[4 + i]) for i in range(HEADS)
+        pltpu.make_async_copy(ob[0].at[i], out_ref.at[:, columns(i)], local_sem.at[4 + i]) for i in range(HEADS)
     ]
 
     def out_copy(k, i, receive):
         return remote(
-            ob[k].at[i], out_hbm.at[:, columns(i)], o_send.at[(k - 1) * HEADS + i], o_recv.at[receive * HEADS + i],
+            ob[k].at[i], out_ref.at[:, columns(i)], o_send.at[(k - 1) * HEADS + i], o_recv.at[receive * HEADS + i],
             mates[k],
         )
 
@@ -448,7 +453,6 @@
 
 
 def layer(plan, collective_id, tokens, norm_gain, w_query, key_weight, value_weight, vertical_blocks, slash_offsets):
-    cosine, sine = rope_tables(lax.axis_index("seq"))
     bf16 = jnp.bfloat16
     unit = (HALF, 2 * HW)
     dma = pltpu.SemaphoreType.DMA
@@ -469,6 +473,7 @@
         + many((HEADS * ROWS, HW))
         + [pltpu.VMEM((10 * ROWS, HW), bf16)] * 2
         + many((HEADS, ROWS, HW))
+        + [pltpu.VMEM((ROWS, HW), jnp.float32)] * 2
         + [dma((4 + HEADS,)), dma((CHUNKS + 1,)), dma((2 * CHUNKS + 1,)), dma((CHUNKS,))]
     )
     for count in (8, 56, 24, 8, 12, 4, 28, 12):
@@ -478,15 +483,22 @@
     hbm = pl.BlockSpec(memory_space=pl.ANY)
     out = pl.pallas_call(
         functools.partial(kernel, plan),
-        out_shape=jax.ShapeDtypeStruct((ROWS, DOCS * HEADS * HW), bf16),
-        in_specs=[smem, smem, hbm, vmem, hbm, hbm, hbm, vmem, vmem],
-        out_specs=hbm,
+        out_shape=pltpu.VMEM((ROWS, DOCS * HEADS * HW), bf16),
+        in_specs=[smem, smem, hbm, vmem, hbm, hbm, hbm] + [vmem] * 4,
+        out_specs=vmem,
         scratch_shapes=scratch,
         compiler_params=pltpu.CompilerParams(
             collective_id=collective_id, has_side_effects=True, vmem_limit_bytes=60 * 1024 * 1024
         ),
     )(
-        vertical_blocks, slash_offsets, tokens[0], norm_gain[None, :], w_query, key_weight, value_weight, cosine, sine
+        vertical_blocks,
+        slash_offsets,
+        tokens[0],
+        norm_gain[None, :],
+        w_query,
+        key_weight,
+        value_weight,
+        *rope_constants(),
     )
     return out[None]
 

time: 91.7 us -> 85.2 us (0.929)
  Pallas kernels: 88.6 us -> 83.4 us
  other arithmetic: 1.08 us -> 0 us
  local copies, waits for them, and re-layouts: 1.88 us -> 0.8 us
    pallas_call x1, Pallas kernels: 88.6 us -> 83.4 us  [layer(): pl.pallas_call(functools.partial(kernel, plan), out_shape=pltpu.VMEM((ROW...]
    unnamed x1, local copies, waits for them, and re-layouts: 1.88 us -> 0.8 us
where the time goes in v6:
time: 85.2 us; the launch traced here: 84.2 us
  Pallas kernels  83.4 us (98%)
    pallas_call x1, Pallas kernels, layer(): pl.pallas_call(functools.partial(kernel, plan), out_shape=pltpu.VMEM((ROW...  83.4 us

profile of v6, /device:TPU:5, one launch (start us, length us, event | category | flops | bytes accessed | tf_op | source)
XLA Modules:
  0.0 84.2 jit_solution(11394799183880827594)
XLA Ops:
  0.0 83.4 %shard_map.109 = bf16[128,2048]{1,0:T(8,128)(2,1)S(1)} custom-call(s32[4,4,4]{2,1,0:T(4,128)} %vert_ref.1, s32[4,4,4]{2,1,0:T(4,128)} %slash_ref.1, bf16[128,4096]{1,0:T(8,128)(2,1)} %bitcast.4, f32[1,4096]{1,0:T(1,128)} %bitcast.5, bf16[4096,512]{1,0:T(8,128)(2,1)} %wq_hbm.1, bf16[4096,128]{1,0:T(8,128)(2,1)} %wk_hbm.1, bf16[4096,128]{1,0:T(8,128)(2,1)} %wv_hbm.1, ...), custom_call_target="tpu_custom_call" | custom-call | tf_op jit(solution)/shard_map/pallas_call | solution.py:484
  83.4 0.8 copy.13

commit v7 on v6

--- a/solution.py
+++ b/solution.py
@@ -201,7 +201,7 @@
         crossing[k - 2][c].land()
         handed[k - 2][c].start()
         handed[k - 2][c].landed = True
-        if k == 2 and c == CHUNKS - 2:
+        if k == 2 and c == CHUNKS - 3:
             for copy in crossing[1]:
                 copy.start()
         norm(k, c * PART, PART)

time: 85.2 us -> 87.2 us (1.023); the launches traced: 84.2 us -> 87.1 us
  Pallas kernels: 83.4 us -> 86.3 us
    pallas_call x1, Pallas kernels: 83.4 us -> 86.3 us  [layer(): pl.pallas_call(functools.partial(kernel, plan), out_shape=pltpu.VMEM((ROW...]
where the time goes in v7:
time: 87.2 us; the launch traced here: 87.1 us
  Pallas kernels  86.3 us (99%)
    pallas_call x1, Pallas kernels, layer(): pl.pallas_call(functools.partial(kernel, plan), out_shape=pltpu.VMEM((ROW...  86.3 us

profile of v7, /device:TPU:5, one launch (start us, length us, event | category | flops | bytes accessed | tf_op | source)
XLA Modules:
  0.0 87.1 jit_solution(8264699423229231779)
XLA Ops:
  0.0 86.3 %shard_map.109 = bf16[128,2048]{1,0:T(8,128)(2,1)S(1)} custom-call(s32[4,4,4]{2,1,0:T(4,128)} %vert_ref.1, s32[4,4,4]{2,1,0:T(4,128)} %slash_ref.1, bf16[128,4096]{1,0:T(8,128)(2,1)} %bitcast.4, f32[1,4096]{1,0:T(1,128)} %bitcast.5, bf16[4096,512]{1,0:T(8,128)(2,1)} %wq_hbm.1, bf16[4096,128]{1,0:T(8,128)(2,1)} %wk_hbm.1, bf16[4096,128]{1,0:T(8,128)(2,1)} %wv_hbm.1, ...), custom_call_target="tpu_custom_call" | custom-call | tf_op jit(solution)/shard_map/pallas_call | solution.py:484
  86.3 0.8 copy.13
